TPU v7x, 256 devices: a whole 4x4x8 slice. The times are simulated.
256 devices in a mesh: sector: 32 (over y, x, core), row: 8 (over z).
Axes of the slice: x: 4, y: 4, z: 8, core: 2. Of those that a mesh axis runs over, the one named last changes fastest.
Arguments:
- environment: bfloat16 [64, 4, 2048, 2048], P('sector', None, None, 'row')
- site_block: bfloat16 [64, 2048, 512], P('sector', 'row'), may hold values from -6 to 6
- next_site: bfloat16 [64, 512, 4096], P('sector', None, 'row'), may hold values from -6 to 6
- charges: int32 [64], replicated, may hold values from -32 to 31, as said below
- sizes: int32 [64], replicated, may hold values from 1024 to 2048, as said below
- pairs: int32 [64, 4], replicated, may hold values from 0 to 63, as said below
- owner: int32 [64], replicated, may hold values from 0 to 63, as said below
Outputs:
- isometry: float32 [2048, 64, 512], P('row', 'sector')
- advanced: bfloat16 [64, 512, 4096], P('sector', None, 'row')
Inputs may be any that keep to these rules, and one draw needn't show every extreme that they name: `owner`: a permutation: every stored block index holds exactly one sector. All charges are distinct. `sizes`: multiples of 128; some sector has exactly 2048 rows and some has exactly 1024. `pairs`: row c lists the sectors whose charges differ from sector c's by -2, -1, 1 and 2, counted cyclically over the 64 charges.
All inputs are finite; a program needn't handle non-finite values.
Results may differ from a plain program's by a relative error of at most 0.0044.
Values may be sent and summed in bfloat16 or wider, within the bound.
A program may use at most 128 MiB of HBM per device.

v0:
```python
import jax
import jax.numpy as jnp
from jax import lax
from jax.sharding import PartitionSpec as P


def lookup(values_table, indices):
    positions = jnp.arange(values_table.shape[0], dtype=jnp.int32)
    return jnp.sum(jnp.where(indices[..., None] == positions, values_table, 0), axis=-1)


def local(environment, site_block, next_site, charges, sizes, pairs, owner):
    per_group, rows_local, window = site_block.shape
    row_count = lax.axis_size("row")
    sector_count = per_group * lax.axis_size("sector")
    capacity = rows_local * row_count
    group_index = lax.axis_index("sector")
    row_index = lax.axis_index("row")
    sector_ids = jnp.arange(sector_count, dtype=jnp.int32)
    my_slots = group_index * per_group + jnp.arange(per_group, dtype=jnp.int32)
    my_sectors = jnp.sum(
        jnp.where(owner[None, :] == my_slots[:, None], sector_ids[None, :], 0), axis=1
    )
    target_size = lookup(sizes, my_sectors)
    chosen = (my_sectors[:, None] == sector_ids[None, :])[:, :, None]
    source_sectors = jnp.sum(jnp.where(chosen, pairs[None, :, :], 0), axis=1)
    source_slots = lookup(owner, source_sectors)
    chem_field = 2.0 * lookup(charges, my_sectors).astype(jnp.float32) / sector_count
    first_row = row_index * rows_local
    local_rows = first_row + jnp.arange(rows_local, dtype=jnp.int32)
    keep_rows = local_rows[None, :] < target_size[:, None]
    site_kept = jnp.where(keep_rows[:, :, None], site_block, jnp.zeros((), site_block.dtype))
    gathered = lax.all_gather(site_kept, "sector", axis=0, tiled=True)
    picked = jnp.take(gathered, source_slots, axis=0)
    local_term = chem_field[None, :, None] * jnp.swapaxes(site_kept, 0, 1).astype(jnp.float32)
    partial_sum = jnp.einsum(
        "ikcr,ikrw->ciw", environment, picked, preferred_element_type=jnp.float32
    )
    own_rows = lax.dynamic_slice_in_dim(partial_sum, first_row, rows_local, 0) + local_term
    partial_sum = lax.dynamic_update_slice_in_dim(partial_sum, own_rows, first_row, 0)
    summed_full = lax.psum(partial_sum, "row")
    all_rows = jnp.arange(capacity, dtype=jnp.int32)
    keep_full = (all_rows[:, None] < target_size[None, :])[:, :, None]
    summed_full = jnp.where(keep_full, summed_full, jnp.zeros((), jnp.float32))
    gram_matrix = jnp.einsum(
        "cis,cit->ist", summed_full, summed_full, precision=lax.Precision.HIGHEST
    )
    bond_rows = lax.dynamic_slice_in_dim(summed_full, first_row, rows_local, 0)
    factor = jnp.linalg.cholesky(gram_matrix)
    blocks_first = jnp.swapaxes(bond_rows, 0, 1)
    solved = lax.linalg.triangular_solve(
        factor, blocks_first, left_side=False, lower=True, transpose_a=True
    )
    isometry = jnp.swapaxes(solved, 0, 1) * jnp.sqrt(target_size.astype(jnp.float32))[None, :, None]
    trace_sum = jnp.trace(gram_matrix, axis1=1, axis2=2)
    scaling = lax.rsqrt(trace_sum / window + 1e-06)
    upper_bf = (jnp.swapaxes(factor, 1, 2) * scaling[:, None, None]).astype(jnp.bfloat16)
    advanced = jnp.einsum(
        "ist,itn->isn", upper_bf, next_site, preferred_element_type=jnp.float32
    ).astype(jnp.bfloat16)
    return (isometry, advanced)


def solution(mesh):
    return jax.shard_map(
        local,
        mesh=mesh,
        in_specs=(
            P("sector", None, None, "row"),
            P("sector", "row", None),
            P("sector", None, "row"),
            P(),
            P(),
            P(),
            P(),
        ),
        out_specs=(P("row", "sector", None), P("sector", None, "row")),
        check_vma=False,
    )
```

profile of v0, /device:TPU:2, one launch (start us, length us, event | category | flops | bytes accessed | tf_op | source)
XLA Modules:
  0.0 619.2 jit_solution(9111537099410155127)
XLA Ops:
  12.1 80.0 %all-gather.2.cloned.1.call-done = bf16[64,256,512]{2,1,0:T(8,128)(2,1)} async-done(((bf16[2,256,512]{2,1,0:T(8,128)(2,1)}), bf16[64,256,512]{2,1,0:T(8,128)(2,1)}) %all-gather.2.cloned.1.call-update) | async-done | bytes 16777232 | tf_op jit(solution)/shard_map/all_gather | solution.py:33
  92.2 6.4 %gather_fusion = bf16[8,256,512]{2,1,0:T(8,128)(2,1)S(1)} fusion(bf16[64,256,512]{2,1,0:T(8,128)(2,1)} %all-gather.2.cloned.1.call-done, s32[1024]{0:T(1024)S(1)} %pad_clamp_fusion), kind=kCustom, calls=%fused_computation | custom fusion | bytes 4194336 | tf_op jit(solution)/shard_map/jit(_take)/gather | solution.py:34
  98.6 2.4 copy.55
  101.0 8.1 %fusion.1 = f32[2,512,2048,1]{2,1,3,0:T(8,128)S(1)} fusion(bf16[2,4,2048,256]{3,2,1,0:T(8,128)(2,1)} %param.7, bf16[2,4,256,512]{2,3,1,0:T(8,128)(2,1)} %copy.55, pred[2,4]{1,0:T(4,128)(4,1)S(1)} %compare_and_fusion), kind=kOutput, calls=%fused_computation.9 | convolution fusion | flops 4296015872 | bytes 18874376 | tf_op jit(solution)/shard_map/ikcr,ikrw->ciw/dot_general | solution.py:36
  109.2 3.2 copy.110
  116.4 185.0 %all-reduce.3.cloned.1.call-done = f32[2048,2,512]{0,2,1:T(8,128)} async-done(((f32[2048,2,512]{0,2,1:T(8,128)}), f32[2048,2,512]{0,2,1:T(8,128)}) %all-reduce.3.cloned.1.call-update) | async-done | bytes 8388624 | tf_op jit(solution)/shard_map/psum | solution.py:41
  301.4 4.3 broadcast_select_fusion
  305.7 13.8 %fusion.47 = f32[2,512,512]{2,1,0:T(8,128)S(1)} fusion(f32[2048,2,512]{0,2,1:T(8,128)S(1)} %broadcast_select_fusion), kind=kOutput, calls=%fused_computation.111 | convolution fusion | flops 12884901888 | bytes 10485760 | tf_op jit(solution)/shard_map/cis,cit->ist/dot_general | solution.py:45
  322.5 2.8 select_reduce_fusion
  326.7 23.5 %custom-call.34 = f32[2,128,128]{2,1,0:T(8,128)S(1)} custom-call(f32[2,128,128]{2,1,0:T(8,128)S(1)} %cholesky.274), custom_call_target="Cholesky" | custom-call | tf_op jit(solution)/shard_map/jit(cholesky)/cholesky | solution.py:49
  350.5 19.7 %custom-call.35 = f32[2,1,128,128]{2,3,1,0:T(8,128)S(1)} custom-call(f32[2,1,128,128]{3,2,1,0:T(8,128)S(1)} %select_bitcast_fusion.2), custom_call_target="InvertDiagBlocksLowerTriangular" | custom-call | tf_op jit(solution)/shard_map/jit(cholesky)/cholesky | solution.py:49
  373.8 25.1 %custom-call.36 = f32[2,128,128]{2,1,0:T(8,128)} custom-call(f32[2,128,128]{2,1,0:T(8,128)} %cholesky.278), custom_call_target="Cholesky" | custom-call | tf_op jit(solution)/shard_map/jit(cholesky)/cholesky | solution.py:49
  400.5 21.1 %custom-call.37 = f32[2,1,128,128]{2,3,1,0:T(8,128)} custom-call(f32[2,1,128,128]{3,2,1,0:T(8,128)} %get-tuple-element.37), custom_call_target="InvertDiagBlocksLowerTriangular" | custom-call | tf_op jit(solution)/shard_map/jit(cholesky)/cholesky | solution.py:49
  425.1 24.9 %custom-call.38 = f32[2,128,128]{2,1,0:T(8,128)} custom-call(f32[2,128,128]{2,1,0:T(8,128)} %cholesky.283), custom_call_target="Cholesky" | custom-call | tf_op jit(solution)/shard_map/jit(cholesky)/cholesky | solution.py:49
  451.6 21.5 %custom-call.39 = f32[2,1,128,128]{2,3,1,0:T(8,128)} custom-call(f32[2,1,128,128]{3,2,1,0:T(8,128)} %get-tuple-element.35), custom_call_target="InvertDiagBlocksLowerTriangular" | custom-call | tf_op jit(solution)/shard_map/jit(cholesky)/cholesky | solution.py:49
  475.8 23.5 %custom-call.40 = f32[2,128,128]{2,1,0:T(8,128)S(1)} custom-call(f32[2,128,128]{2,1,0:T(8,128)S(1)} %convolution_subtract_fusion.5), custom_call_target="Cholesky" | custom-call | tf_op jit(solution)/shard_map/jit(cholesky)/cholesky | solution.py:49
  501.3 2.7 fusion.4
  504.0 14.3 %while.1 = (s32[]{:T(128)}, f32[2,512,512]{2,1,0:T(8,128)}, s32[4,2]{0,1:T(2,128)S(1)}, f32[4,2,128,128]{3,2,0,1:T(8,128)}, s32[]{:T(128)}) while((s32[]{:T(128)}, f32[2,512,512]{2,1,0:T(8,128)}, s32[4,2]{0,1:T(2,128)S(1)}, f32[4,2,128,128]{3,2,0,1:T(8,128)}, s32[]{:T(128)}) %tuple.37), condition=%wide.while_cond, body=%wide.while_body.sunk | while | flops 2 | bytes 263777 | solution.py:51
  504.6 3.0 bitcast_dynamic-update-slice_fusion.2
  508.2 3.0 bitcast_dynamic-update-slice_fusion.2
  511.8 3.0 bitcast_dynamic-update-slice_fusion.2
  515.4 2.9 bitcast_dynamic-update-slice_fusion.2
  518.3 80.2 %custom-call.41 = f32[2,4,128,128]{2,3,1,0:T(8,128)} custom-call(f32[2,4,128,128]{3,2,1,0:T(8,128)} %bitcast.83), custom_call_target="InvertDiagBlocksLowerTriangular" | custom-call | tf_op jit(solution)/shard_map/triangular_solve | solution.py:51
  608.0 2.2 copy.80
  (93 shorter events, 42.3 us)
Async XLA Ops:
  7.2 603.1 %copy-start = (bf16[2,512,512]{2,1,0:T(8,128)(2,1)S(1)}, bf16[2,512,512]{2,1,0:T(8,128)(2,1)}, u32[]{:S(2)}) copy-start(bf16[2,512,512]{2,1,0:T(8,128)(2,1)} %param.9) | copy-start | bytes 3145732
  7.2 4.6 copy-start.11
  7.2 4.5 copy-start.9
  7.2 85.0 %all-gather.2.cloned.1.call-start = ((), (), s32[]{:S(2)}) async-start(), calls=%async_computation | async-start | bytes 17301504 | tf_op jit(solution)/shard_map/all_gather | solution.py:33
  8.6 3.5 copy-start.2
  11.5 289.9 %all-reduce.3.cloned.1.call-start = ((), (), s32[]{:S(2)}) async-start(), calls=%async_computation.1 | async-start | bytes 16777216 | tf_op jit(solution)/shard_map/psum | solution.py:41
  109.1 3.2 copy-start.3
  325.3 1.4 copy-start.1
  350.2 21.5 %copy-start.5 = (f32[2,128,128]{2,1,0:T(8,128)}, f32[2,128,128]{2,1,0:T(8,128)S(1)}, u32[]{:S(2)}) copy-start(f32[2,128,128]{2,1,0:T(8,128)S(1)} %custom-call.34) | copy-start | bytes 393220
  422.8 77.1 %copy-start.6 = (f32[2,128,128]{2,1,0:T(8,128)S(1)}, f32[2,128,128]{2,1,0:T(8,128)}, u32[]{:S(2)}) copy-start(f32[2,128,128]{2,1,0:T(8,128)} %copy-done.5) | copy-start | bytes 393220
  501.3 2.7 copy-start.12
  598.5 4.3 copy-start.4
  598.5 5.8 copy-start.8
  602.8 4.0 copy-start.10
  606.9 3.4 copy-start.7
Sparse Core Ops, SparseCore 0:
  11.6 80.4 all-gather.1
  113.9 187.4 all-reduce.2
where the time goes:
time: 623 us; the launch traced here: 619 us
  waiting for transfers between devices  265 us (43%)
  other arithmetic  262 us (42%)
  matrix products  40.7 us (7%)
  local copies, waits for them, and re-layouts  37 us (6%)
  between operations  14.6 us (2%)
    psum x1, waiting for transfers between devices, local(): summed_full = lax.psum(partial_sum, 'row')  185 us
    another operation x16, other arithmetic, local(): factor = jnp.linalg.cholesky(gram_matrix)  164 us
    another operation x4, other arithmetic, local(): lax.linalg.triangular_solve(factor, blocks_first, left_side=False, lower=...  84.1 us
    all_gather x1, waiting for transfers between devices, local(): gathered = lax.all_gather(site_kept, 'sector', axis=0, tiled=True)  80 us
    another operation x12, local copies, waits for them, and re-layouts  14.3 us
    dot_general x1, matrix products, local(): jnp.einsum('cis,cit->ist', summed_full, summed_full, precision=lax.Precis...  13.8 us
  transfers between devices with their start and end apart: 2, of which 2 were waited for; matrix products, arithmetic and copies ran while one was open for 1% of the time, Pallas kernels for 0%

commit v1 on v0

v1 whole, which is shorter than its diff:
```python
import jax
import jax.numpy as jnp
from jax import lax
from jax.experimental import pallas as pl
from jax.experimental.pallas import tpu as pltpu
from jax.sharding import PartitionSpec as P

NB = 4
T = 128
GROUP = 4
HI = lax.Precision.HIGHEST
PAIRS = [(p, i) for p in range(NB) for i in range(p, NB)]


def dot(a, b, dims, precision=HI):
    return lax.dot_general(
        a, b, (dims, ((), ())), precision=precision, preferred_element_type=jnp.float32
    )


def factor_tiles(a_tiles, u_ref, w_ref):
    count = len(a_tiles)
    rows8 = T // 8
    lane = lax.broadcasted_iota(jnp.int32, (8, T), 1)
    sub = lax.broadcasted_iota(jnp.int32, (8, T), 0)
    w_tiles = [
        [jnp.where(lane == sub + 8 * i, 1.0, 0.0).astype(jnp.float32) for i in range(rows8)]
        for _ in range(count)
    ]

    def spread(x, s):
        return jnp.broadcast_to(x[s : s + 1, :], (8, T))

    for j0 in range(0, T, GROUP):
        g = j0 // 8
        s0 = j0 - 8 * g
        state = []
        for m in range(count):
            cols = [
                [
                    jnp.broadcast_to(a_tiles[m][i][:, j0 + k : j0 + k + 1], (8, T))
                    for i in range(g, rows8)
                ]
                for k in range(GROUP)
            ]
            rows = [spread(a_tiles[m][g], s0 + k) for k in range(GROUP)]
            wrows = [spread(w_tiles[m][g], s0 + k) for k in range(GROUP)]
            state.append((cols, rows, wrows))
        for k in range(GROUP):
            for m in range(count):
                cols, rows, wrows = state[m]
                rs = lax.rsqrt(spread(cols[k][0], s0 + k))
                cols[k] = [c * rs for c in cols[k]]
                rows[k] = rows[k] * rs
                wrows[k] = wrows[k] * rs
                for q in range(k + 1, GROUP):
                    f = spread(cols[k][0], s0 + q)
                    cols[q] = [c - l * f for c, l in zip(cols[q], cols[k])]
                    rows[q] = rows[q] - rows[k] * f
                    wrows[q] = wrows[q] - wrows[k] * f
        for m in range(count):
            cols, rows, wrows = state[m]
            for k in range(GROUP):
                j = j0 + k
                keep = lane[:1] >= j
                u_ref[m, j : j + 1, :] = jnp.where(keep, rows[k][:1], 0.0)
                w_ref[m, j : j + 1, :] = wrows[k][:1]
            last = s0 + GROUP == 8
            for i in range(g + 1 if last else g, rows8):
                a, w = a_tiles[m][i], w_tiles[m][i]
                for k in range(GROUP):
                    l = cols[k][i - g]
                    if i == g:
                        l = jnp.where(sub >= s0 + GROUP, l, 0.0)
                    a = a - l * rows[k]
                    w = w - l * wrows[k]
                a_tiles[m][i], w_tiles[m][i] = a, w


def tail_kernel(g_ref, b_ref, next_ref, root_ref, iso_ref, adv_ref, s_ref, d_ref, u_ref, w_ref):
    count = g_ref.shape[0]
    eye = lax.broadcasted_iota(jnp.int32, (T, T), 0) == lax.broadcasted_iota(jnp.int32, (T, T), 1)
    scales = []
    for m in range(count):
        trace = jnp.zeros((), jnp.float32)
        for n, (p, i) in enumerate(PAIRS):
            s_ref[m, p, i] = g_ref[m, n]
            if p == i:
                trace = trace + jnp.sum(jnp.where(eye, g_ref[m, n], 0.0))
        scales.append(lax.rsqrt(jnp.full((1, T), trace / (NB * T) + 1e-6, jnp.float32)))

    def block(p, carry):
        tiles = [[s_ref[m, p, p, 8 * i : 8 * i + 8, :] for i in range(T // 8)] for m in range(count)]
        factor_tiles(tiles, u_ref, w_ref)
        for m in range(count):
            d_ref[m, p] = w_ref[m]
            s_ref[m, p, p] = u_ref[m]

        def panel(i, c):
            for m in range(count):
                s_ref[m, p, i] = dot(w_ref[m], s_ref[m, p, i], ((1,), (0,)))
            return c

        lax.fori_loop(p + 1, NB, panel, 0)

        def trail(i, c):
            def inner(k, c2):
                for m in range(count):
                    s_ref[m, i, k] = s_ref[m, i, k] - dot(s_ref[m, p, i], s_ref[m, p, k], ((0,), (0,)))
                return c2

            return lax.fori_loop(i, NB, inner, c)

        lax.fori_loop(p + 1, NB, trail, 0)
        return carry

    lax.fori_loop(0, NB, block, 0)
    for m in range(count):
        solved = []
        for j in range(NB):
            x = b_ref[m, :, T * j : T * j + T]
            for i in range(j):
                x = x - dot(solved[i], s_ref[m, i, j], ((1,), (0,)))
            x = dot(x, d_ref[m, j], ((1,), (1,)))
            solved.append(x)
            iso_ref[m, :, T * j : T * j + T] = x * root_ref[m]
        for p in range(NB):
            total = None
            for i in range(p, NB):
                up = (s_ref[m, p, i] * scales[m]).astype(jnp.bfloat16)
                term = dot(up, next_ref[m, T * i : T * i + T, :], ((1,), (0,)), None)
                total = term if total is None else total + term
            adv_ref[m, T * p : T * p + T, :] = total.astype(jnp.bfloat16)


def tail(gram, bond, next_site, root):
    count, rows, window = bond.shape
    vmem = pl.BlockSpec(memory_space=pltpu.VMEM)
    return pl.pallas_call(
        tail_kernel,
        out_shape=(
            jax.ShapeDtypeStruct((count, rows, window), jnp.float32),
            jax.ShapeDtypeStruct(next_site.shape, jnp.bfloat16),
        ),
        in_specs=[vmem] * 4,
        out_specs=(vmem, vmem),
        scratch_shapes=[
            pltpu.VMEM((count, NB, NB, T, T), jnp.float32),
            pltpu.VMEM((count, NB, T, T), jnp.float32),
            pltpu.VMEM((count, T, T), jnp.float32),
            pltpu.VMEM((count, T, T), jnp.float32),
        ],
        compiler_params=pltpu.CompilerParams(vmem_limit_bytes=40 * 1024 * 1024),
        name="tail",
    )(gram, bond, next_site, root)


def lookup(values_table, indices):
    positions = jnp.arange(values_table.shape[0], dtype=jnp.int32)
    return jnp.sum(jnp.where(indices[..., None] == positions, values_table, 0), axis=-1)


def local(environment, site_block, next_site, charges, sizes, pairs, owner):
    per_group, rows_local, window = site_block.shape
    sector_count = per_group * lax.axis_size("sector")
    group_index = lax.axis_index("sector")
    row_index = lax.axis_index("row")
    sector_ids = jnp.arange(sector_count, dtype=jnp.int32)
    my_slots = group_index * per_group + jnp.arange(per_group, dtype=jnp.int32)
    my_sectors = jnp.sum(
        jnp.where(owner[None, :] == my_slots[:, None], sector_ids[None, :], 0), axis=1
    )
    target_size = lookup(sizes, my_sectors)
    chosen = (my_sectors[:, None] == sector_ids[None, :])[:, :, None]
    source_sectors = jnp.sum(jnp.where(chosen, pairs[None, :, :], 0), axis=1)
    source_slots = lookup(owner, source_sectors)
    chem_field = 2.0 * lookup(charges, my_sectors).astype(jnp.float32) / sector_count
    root = jnp.sqrt(target_size.astype(jnp.float32))
    local_rows = row_index * rows_local + jnp.arange(rows_local, dtype=jnp.int32)
    keep_rows = (local_rows[None, :] < target_size[:, None])[:, :, None]
    site_kept = jnp.where(keep_rows, site_block, jnp.zeros((), site_block.dtype))
    gathered = lax.all_gather(site_kept, "sector", axis=0, tiled=True)
    picked = jnp.take(gathered, source_slots, axis=0)
    partial_sum = jnp.einsum(
        "ikcr,ikrw->icw", environment, picked, preferred_element_type=jnp.float32
    ).astype(jnp.bfloat16)
    summed = lax.psum_scatter(partial_sum, "row", scatter_dimension=1, tiled=True)
    bond = summed.astype(jnp.float32) + chem_field[:, None, None] * site_kept.astype(jnp.float32)
    bond = jnp.where(keep_rows, bond, 0.0)
    part = jnp.einsum("iws,iwt->ist", bond, bond, precision=HI)
    packed = jnp.stack(
        [part[:, T * p : T * p + T, T * i : T * i + T] for p, i in PAIRS], axis=1
    )
    packed = lax.psum(packed, "row")
    wide_root = jnp.broadcast_to(root[:, None, None], (per_group, 1, T))
    iso, advanced = tail(packed, bond, next_site, wide_root)
    return (jnp.swapaxes(iso, 0, 1), advanced)


def solution(mesh):
    return jax.shard_map(
        local,
        mesh=mesh,
        in_specs=(
            P("sector", None, None, "row"),
            P("sector", "row", None),
            P("sector", None, "row"),
            P(),
            P(),
            P(),
            P(),
        ),
        out_specs=(P("row", "sector", None), P("sector", None, "row")),
        check_vma=False,
    )
```

time: 623 us -> 299 us (0.48)
  other arithmetic: 262 us -> 6.92 us
  waiting for transfers between devices: 265 us -> 210 us
  Pallas kernels: 0 us -> 41.8 us
  matrix products: 40.7 us -> 12.5 us
  local copies, waits for them, and re-layouts: 37 us -> 13.4 us
    another operation x20 -> x0, other arithmetic: 248 us -> none  [the longest x16 164 us: local(): factor = jnp.linalg.cholesky(gram_matrix)]
    psum x1, waiting for transfers between devices: 185 us -> 75.9 us  [local(): packed = lax.psum(packed, 'row')]
    reduce_scatter x0 -> x1, waiting for transfers between devices: none -> 55 us  [local(): lax.psum_scatter(partial_sum, 'row', scatter_dimension=1, tiled=True)]
    pallas_call x0 -> x1, Pallas kernels: none -> 41.8 us  [tail(): pl.pallas_call(tail_kernel, out_shape=(jax.ShapeDtypeStruct((count, rows,...]
    another operation x13 -> x0, matrix products: 16.8 us -> none  [the longest x6 8.56 us: local(): factor = jnp.linalg.cholesky(gram_matrix)]
    another operation x17 -> x1, local copies, waits for them, and re-layouts: 15.9 us -> 0.02 us  [local(): jnp.stack([part[:, T * p:T * p + T, T * i:T * i + T] for p, i in PAIRS],...]
    dot_general x3 -> x2, matrix products: 23.9 us -> 12.5 us  [the longest x1 10.6 us: local(): jnp.einsum('ikcr,ikrw->icw', environment, picked, preferred_element_type=...]
  transfers between devices with their start and end apart: 2 -> 3, of which waited for: 2 -> 3; matrix products, arithmetic and copies ran while one was open for 1% -> 1% of each run, Pallas kernels for 0% -> 0%
where the time goes in v1:
time: 299 us; the launch traced here: 298 us
  waiting for transfers between devices  210 us (70%)
  Pallas kernels  41.8 us (14%)
  between operations  13.9 us (5%)
  local copies, waits for them, and re-layouts  13.4 us (4%)
  matrix products  12.5 us (4%)
  other arithmetic  6.92 us (2%)
    all_gather x1, waiting for transfers between devices, local(): gathered = lax.all_gather(site_kept, 'sector', axis=0, tiled=True)  78.7 us
    psum x1, waiting for transfers between devices, local(): packed = lax.psum(packed, 'row')  75.9 us
    reduce_scatter x1, waiting for transfers between devices, local(): lax.psum_scatter(partial_sum, 'row', scatter_dimension=1, tiled=True)  55 us
    pallas_call x1, Pallas kernels, tail(): pl.pallas_call(tail_kernel, out_shape=(jax.ShapeDtypeStruct((count, rows,...  41.8 us
    dot_general x1, matrix products, local(): jnp.einsum('ikcr,ikrw->icw', environment, picked, preferred_element_type=...  10.6 us
    gather x2, local copies, waits for them, and re-layouts, local(): picked = jnp.take(gathered, source_slots, axis=0)  8.84 us
  transfers between devices with their start and end apart: 3, of which 3 were waited for; matrix products, arithmetic and copies ran while one was open for 1% of the time, Pallas kernels for 0%

profile of v1, /device:TPU:2, one launch (start us, length us, event | category | flops | bytes accessed | tf_op | source)
XLA Modules:
  0.0 298.3 jit_solution(15382136779047923192)
XLA Ops:
  7.2 0.0 all-gather.2.cloned.1.call-start
  7.2 0.8 fusion.14
  8.1 0.9 select_reduce_fusion.2
  9.0 0.1 broadcast_compare_fusion
  9.0 2.0 broadcast_select_fusion
  11.0 0.0 reduce-scatter.2.cloned.1.call-start
  11.1 0.1 iota_compare_fusion.1
  11.2 0.8 select_reduce_fusion.1
  12.0 0.9 select_reduce_fusion
  12.9 0.1 reshape.93
  13.0 78.7 %all-gather.2.cloned.1.call-done = bf16[64,256,512]{2,1,0:T(8,128)(2,1)} async-done(((bf16[2,256,512]{2,1,0:T(8,128)(2,1)}), bf16[64,256,512]{2,1,0:T(8,128)(2,1)}) %all-gather.2.cloned.1.call-update) | async-done | bytes 16777232 | tf_op jit(solution)/shard_map/all_gather | solution.py:182
  91.7 6.4 %gather_fusion = bf16[8,256,512]{2,1,0:T(8,128)(2,1)S(1)} fusion(bf16[64,256,512]{2,1,0:T(8,128)(2,1)} %all-gather.2.cloned.1.call-done, s32[1024]{0:T(1024)S(1)} %pad_clamp_fusion), kind=kCustom, calls=%fused_computation | custom fusion | bytes 4194336 | tf_op jit(solution)/shard_map/jit(_take)/gather | solution.py:183
  98.1 2.4 copy.19
  100.5 10.6 %fusion = bf16[2,2048,512]{2,1,0:T(8,128)(2,1)} fusion(bf16[2,4,2048,256]{3,2,1,0:T(8,128)(2,1)} %param.7, bf16[2,4,256,512]{2,3,1,0:T(8,128)(2,1)} %copy.19, pred[2,4]{1,0:T(4,128)(4,1)S(1)} %compare_and_fusion), kind=kOutput, calls=%fused_computation.2 | convolution fusion | flops 4298113024 | bytes 14680072 | tf_op jit(solution)/shard_map/ikcr,ikrw->icw/dot_general | solution.py:184
  111.1 0.0 all-reduce.2.cloned.1.call-start
  111.2 55.0 %reduce-scatter.2.cloned.1.call-done = bf16[2,256,512]{2,1,0:T(8,128)(2,1)} async-done(((bf16[2,2048,512]{2,1,0:T(8,128)(2,1)}), bf16[2,256,512]{2,1,0:T(8,128)(2,1)}) %reduce-scatter.2.cloned.1.call-update) | async-done | bytes 524304 | tf_op jit(solution)/shard_map/reduce_scatter | solution.py:187
  166.2 1.3 add_select_fusion.b_ref
  167.5 1.9 fusion.16
  169.8 1.1 copy-done.3
  170.9 75.9 %all-reduce.2.cloned.1.call-done.g_ref = f32[2,10,128,128]{3,2,1,0:T(8,128)} async-done(((f32[2,10,128,128]{3,2,1,0:T(8,128)}), f32[2,10,128,128]{3,2,1,0:T(8,128)}) %all-reduce.2.cloned.1.call-update) | async-done | bytes 1310736 | tf_op jit(solution)/shard_map/psum | solution.py:194
  246.7 0.1 broadcast_in_dim.122.root_ref
  246.8 1.3 copy-done
  248.1 41.8 %tail.1 = (f32[2,256,512]{2,1,0:T(8,128)S(1)}, bf16[2,512,512]{2,1,0:T(8,128)(2,1)}) custom-call(f32[2,10,128,128]{3,2,1,0:T(8,128)S(1)} %copy-done, f32[2,256,512]{2,1,0:T(8,128)S(1)} %add_select_fusion.b_ref, bf16[2,512,512]{2,1,0:T(8,128)(2,1)S(1)} %copy-done.1, f32[2,1,128]{2,1,0:T(1,128)S(1)} %broadcast_in_dim.122.root_ref), custom_call_target="tpu_custom_call" | custom-call | tf_op jit(solution)/shard_map/tail/pallas_call | solution.py:139
  290.0 1.8 copy.22
  (26 shorter events, 0.3 us)
Async XLA Ops:
  7.2 84.5 %all-gather.2.cloned.1.call-start = ((), (), s32[]{:S(2)}) async-start(), calls=%async_computation.1 | async-start | bytes 17301504 | tf_op jit(solution)/shard_map/all_gather | solution.py:182
  11.0 155.1 %reduce-scatter.2.cloned.1.call-start = ((), (), s32[]{:S(2)}) async-start(), calls=%async_computation.2 | async-start | bytes 4718592 | tf_op jit(solution)/shard_map/reduce_scatter | solution.py:187
  111.1 55.1 %copy-start.2 = (bf16[2,256,512]{2,1,0:T(8,128)(2,1)S(1)}, bf16[2,256,512]{2,1,0:T(8,128)(2,1)}, u32[]{:S(2)}) copy-start(bf16[2,256,512]{2,1,0:T(8,128)(2,1)} %param.8) | copy-start | bytes 1572868
  111.1 135.6 %all-reduce.2.cloned.1.call-start = ((), (), s32[]{:S(2)}) async-start(), calls=%async_computation.3 | async-start | bytes 2621440 | tf_op jit(solution)/shard_map/psum | solution.py:194
  169.5 77.4 %copy-start.1 = (bf16[2,512,512]{2,1,0:T(8,128)(2,1)S(1)}, bf16[2,512,512]{2,1,0:T(8,128)(2,1)}, u32[]{:S(2)}) copy-start(bf16[2,512,512]{2,1,0:T(8,128)(2,1)} %next_ref.1) | copy-start | bytes 3145732
  169.7 1.1 copy-start.3
  246.8 1.3 copy-start
Sparse Core Ops, SparseCore 0:
  11.2 80.4 all-gather.1
  111.3 54.8 reduce-scatter.1
  171.0 75.7 all-reduce.1

commit v2 on v1

--- a/solution.py
+++ b/solution.py
@@ -78,15 +78,16 @@
 
 
 def tail_kernel(g_ref, b_ref, next_ref, root_ref, iso_ref, adv_ref, s_ref, d_ref, u_ref, w_ref):
-    count = g_ref.shape[0]
+    count = b_ref.shape[0]
     eye = lax.broadcasted_iota(jnp.int32, (T, T), 0) == lax.broadcasted_iota(jnp.int32, (T, T), 1)
     scales = []
     for m in range(count):
         trace = jnp.zeros((), jnp.float32)
         for n, (p, i) in enumerate(PAIRS):
-            s_ref[m, p, i] = g_ref[m, n]
+            for q in range(T // 16):
+                s_ref[m, p, i, 16 * q : 16 * q + 16, :] = g_ref[q, m, n]
             if p == i:
-                trace = trace + jnp.sum(jnp.where(eye, g_ref[m, n], 0.0))
+                trace = trace + jnp.sum(jnp.where(eye, s_ref[m, p, i], 0.0))
         scales.append(lax.rsqrt(jnp.full((1, T), trace / (NB * T) + 1e-6, jnp.float32)))
 
     def block(p, carry):
@@ -155,6 +156,320 @@
     )(gram, bond, next_site, root)
 
 
+CHUNKS = 4
+NZ = 8
+SIDE = 4
+ROWS = 256
+MESH = pl.DeviceIdType.MESH
+FLOWS = [(0, 0), (1, 1), (0, 1), (1, 0)]
+
+
+def first_hop(direction, t):
+    return 1 if direction == t else 2
+
+
+def ordered(tasks):
+    rate = {"x": 47.0, "y": 47.0, "z": 47.0, "c": 300.0}
+    link_free, arrival, done, order = {}, {}, set(), []
+    now, left = 0.0, list(tasks)
+    while left:
+        best = None
+        for n, task in enumerate(left):
+            if all(a in done for a in task["after"]) and all(k in arrival for k in task["needs"]):
+                start = max([now] + [arrival[k] for k in task["needs"]])
+                if best is None or start < best[0]:
+                    best = (start, n)
+        start, n = best
+        task = left.pop(n)
+        now = start + task["time"]
+        for key, link, kib in task["sends"]:
+            begin = max(now, link_free.get(link, 0.0))
+            link_free[link] = begin + kib / rate[link[0]]
+            arrival[key] = link_free[link] + (1.0 if link[0] == "c" else 1.8)
+        done.add(task["name"])
+        order.append(task)
+    return order
+
+
+def bond_kernel(
+    src_ref, env_ref, site_ref, extra_ref, keep_ref, bond_ref, gram_ref,
+    g0, g1, g2, g3, env_v, part, send_b, recv_b, gp, gsend, grecv, gfull,
+    env_sem, own_sem, ag_send, ag_recv, rs_send, rs_recv, gr_send, gr_recv, gg_send, gg_recv,
+):
+    gath = (g0, g1, g2, g3)
+    sector, z = lax.axis_index("sector"), lax.axis_index("row")
+    c = sector % 2
+    x = (sector // 2) % SIDE
+    y = sector // (2 * SIDE)
+
+    def at(xx, yy, cc):
+        return {"sector": ((yy % SIDE) * SIDE + xx % SIDE) * 2 + cc}
+
+    def along(m, dmaj, dmin):
+        return at(x + dmin, y + dmaj, c) if m == 0 else at(x + dmaj, y + dmin, c)
+
+    major, minor = (y, x), (x, y)
+    partner = at(x, y, 1 - c)
+    up, down = {"row": (z + 1) % NZ}, {"row": (z + NZ - 1) % NZ}
+
+    def slot(m, maj, mino):
+        return 32 * m + ((maj % SIDE) * 2 + c) * SIDE + mino % SIDE
+
+    barrier = pltpu.get_barrier_semaphore()
+    env_copy = pltpu.make_async_copy(env_ref, env_v, env_sem)
+    env_copy.start()
+    own = []
+    for j in range(CHUNKS):
+        for m in range(2):
+            own.append(
+                pltpu.make_async_copy(
+                    site_ref.at[j, m], gath[j].at[slot(m, major[m], minor[m])], own_sem.at[j, m]
+                )
+            )
+            own[-1].start()
+    partners = [along(0, 0, 1), along(0, 0, 3), along(0, 1, 0), along(0, 3, 0), partner, up, down]
+    for device in partners:
+        pl.semaphore_signal(barrier, inc=1, device_id=device, device_id_type=MESH)
+    pl.semaphore_wait(barrier, len(partners))
+
+    copies = {}
+
+    def send(key, src, dst, ssem, rsem, device):
+        copy = pltpu.make_async_remote_copy(
+            src_ref=src, dst_ref=dst, send_sem=ssem, recv_sem=rsem, device_id=device, device_id_type=MESH
+        )
+        copy.start()
+        copies[key] = copy
+
+    def ag_send_one(j, m, n, ref, device, src=None):
+        send((j, m, n), ref if src is None else src, ref, ag_send.at[j, m, n], ag_recv.at[j, m, n], device)
+
+    def a1(j):
+        for m in range(2):
+            ref = gath[j].at[slot(m, major[m], minor[m])]
+            ag_send_one(j, m, 0, ref, along(m, 0, 1), site_ref.at[j, m])
+            ag_send_one(j, m, 1, ref, along(m, 0, 3), site_ref.at[j, m])
+
+    def a2(j):
+        for m in range(2):
+            copies[j, m, 0].wait_recv()
+            low = gath[j].at[slot(m, major[m], minor[m] + 3), pl.ds(0, ROWS // 2)]
+            ag_send_one(j, m, 2, low, along(m, 0, 1))
+            copies[j, m, 1].wait_recv()
+            high = gath[j].at[slot(m, major[m], minor[m] + 1), pl.ds(ROWS // 2, ROWS // 2)]
+            ag_send_one(j, m, 3, high, along(m, 0, 3))
+
+    def group(j, m, dmaj, start=0, size=SIDE):
+        return gath[j].at[pl.ds(slot(m, major[m] + dmaj, 0) + start, size)]
+
+    def b1(j):
+        for m in range(2):
+            own[2 * j + m].wait()
+            copies[j, m, 2].wait_recv()
+            copies[j, m, 3].wait_recv()
+            ag_send_one(j, m, 4, group(j, m, 0), along(m, 1, 0))
+            ag_send_one(j, m, 5, group(j, m, 0), along(m, 3, 0))
+            ag_send_one(j, m, 8, group(j, m, 0), partner)
+
+    def b2(j):
+        for m in range(2):
+            copies[j, m, 4].wait_recv()
+            ag_send_one(j, m, 6, group(j, m, 3, 0, 2), along(m, 1, 0))
+            copies[j, m, 5].wait_recv()
+            ag_send_one(j, m, 7, group(j, m, 1, 2, 2), along(m, 3, 0))
+            ag_send_one(j, m, 9, group(j, m, 3), partner)
+            ag_send_one(j, m, 10, group(j, m, 1), partner)
+
+    def b3(j):
+        for m in range(2):
+            copies[j, m, 6].wait_recv()
+            copies[j, m, 7].wait_recv()
+            ag_send_one(j, m, 11, group(j, m, 2), partner)
+
+    def ready(j):
+        for m in range(2):
+            for n in (8, 9, 10, 11):
+                copies[j, m, n].wait_recv()
+        if j == 0:
+            env_copy.wait()
+
+    def multiply(j, r):
+        def one(n, carry):
+            t = n % 2
+            o = (n // 2) * (NZ - 2 * r) + r
+            first = pl.multiple_of(((z + o) % NZ) * ROWS, ROWS)
+            total = None
+            for k in range(4):
+                term = jnp.dot(
+                    env_v[t, k, pl.ds(first, ROWS), :],
+                    gath[j][src_ref[t, k]],
+                    preferred_element_type=jnp.float32,
+                )
+                total = term if total is None else total + term
+            part[j, o, t] = total
+            return carry
+
+        lax.fori_loop(0, 2 if r in (0, 4) else 4, one, 0)
+
+    def hop(j, s, direction, t):
+        o = 5 - s if direction == 0 else 3 + s
+        value = part[j, o, t]
+        if s > first_hop(direction, t):
+            copies["r", j, s - 1, direction, t].wait_recv()
+            value = value + recv_b[j, direction, t, s - 2].astype(jnp.float32)
+        send_b[j, direction, t, s - 1] = value.astype(jnp.bfloat16)
+        send(
+            ("r", j, s, direction, t),
+            send_b.at[j, direction, t, s - 1],
+            recv_b.at[j, direction, t, s - 1],
+            rs_send.at[j, direction, t, s - 1],
+            rs_recv.at[j, direction, t, s - 1],
+            up if direction == 0 else down,
+        )
+
+    def finish(j, t):
+        copies["r", j, 4, 0, t].wait_recv()
+        copies["r", j, 4, 1, t].wait_recv()
+        cols = pl.ds(T * j, T)
+        total = part[j, 0, t] + extra_ref[t, :, cols]
+        total = total + recv_b[j, 0, t, 3].astype(jnp.float32) + recv_b[j, 1, t, 3].astype(jnp.float32)
+        bond_ref[t, :, cols] = jnp.where(keep_ref[t] > 0.5, total, 0.0)
+
+    def grams(j):
+        for t in range(2):
+            for i in range(j + 1):
+                value = dot(bond_ref[t, :, T * i : T * i + T], bond_ref[t, :, T * j : T * j + T], ((0,), (0,)))
+                n = PAIRS.index((i, j))
+                for q in range(NZ):
+                    gp[q, t, n] = value[16 * q : 16 * q + 16]
+
+    tasks = []
+
+    def task(name, emit, time, needs=(), after=(), sends=()):
+        tasks.append(dict(name=name, emit=emit, time=time, needs=needs, after=after, sends=sends))
+
+    def axes(m):
+        return ("x", "y") if m == 0 else ("y", "x")
+
+    for j in range(CHUNKS):
+        ms = range(2)
+        mins, majs = [axes(m)[0] for m in ms], [axes(m)[1] for m in ms]
+        task(("a1", j), lambda j=j: a1(j), 0.1, after=[("b1", j - 1)] if j else [],
+             sends=[((j, m, n), mins[m] + str(n), 64) for m in ms for n in (0, 1)])
+        task(("a2", j), lambda j=j: a2(j), 0.1, needs=[(j, m, n) for m in ms for n in (0, 1)],
+             sends=[((j, m, n + 2), mins[m] + str(n), 32) for m in ms for n in (0, 1)])
+        task(("b1", j), lambda j=j: b1(j), 0.1, needs=[(j, m, n) for m in ms for n in (2, 3)],
+             after=[("b2", j - 1)] if j else [],
+             sends=[((j, m, n + 4), majs[m] + str(n), 256) for m in ms for n in (0, 1)]
+             + [((j, m, 8), "c", 256) for m in ms])
+        task(("b2", j), lambda j=j: b2(j), 0.1, needs=[(j, m, n) for m in ms for n in (4, 5)],
+             sends=[((j, m, n + 6), majs[m] + str(n), 128) for m in ms for n in (0, 1)]
+             + [((j, m, n), "c", 256) for m in ms for n in (9, 10)])
+        task(("b3", j), lambda j=j: b3(j), 0.1, needs=[(j, m, n) for m in ms for n in (6, 7)],
+             sends=[((j, m, 11), "c", 256) for m in ms])
+        task(("ready", j), lambda j=j: ready(j), 0.1, needs=[(j, m, n) for m in ms for n in (8, 9, 10, 11)])
+        before = ("ready", j)
+        for r in (4, 3, 2, 1, 0):
+            task(("mm", j, r), lambda j=j, r=r: multiply(j, r), 0.4 if r in (0, 4) else 0.8, after=[before])
+            before = ("mm", j, r)
+            if r == 0:
+                continue
+            s = 5 - r
+            for direction, t in FLOWS:
+                if s >= first_hop(direction, t):
+                    more = s > first_hop(direction, t)
+                    task(("hop", j, s, direction, t),
+                         lambda j=j, s=s, direction=direction, t=t: hop(j, s, direction, t), 0.1,
+                         needs=[("r", j, s - 1, direction, t)] if more else [], after=[before],
+                         sends=[(("r", j, s, direction, t), "z" + str(direction), 64)])
+        for t in range(2):
+            task(("finish", j, t), lambda j=j, t=t: finish(j, t), 0.1,
+                 needs=[("r", j, 4, 0, t), ("r", j, 4, 1, t)], after=[("mm", j, 0)])
+        task(("gram", j), lambda j=j: grams(j), 0.4 + 0.4 * j,
+             after=[("finish", j, 0), ("finish", j, 1)] + ([("gram", j - 1)] if j else []))
+    for item in ordered(tasks):
+        item["emit"]()
+
+    for s in range(1, 5):
+        for direction, t in FLOWS:
+            if s < first_hop(direction, t):
+                continue
+            o = 5 - s if direction == 0 else 3 + s
+            value = gp[(z + o) % NZ, t]
+            if s > first_hop(direction, t):
+                copies["g", s - 1, direction, t].wait_recv()
+                value = value + grecv[direction, t, s - 2]
+            gsend[direction, t, s - 1] = value
+            send(
+                ("g", s, direction, t), gsend.at[direction, t, s - 1], grecv.at[direction, t, s - 1],
+                gr_send.at[direction, t, s - 1], gr_recv.at[direction, t, s - 1],
+                up if direction == 0 else down,
+            )
+    for t in range(2):
+        copies["g", 4, 0, t].wait_recv()
+        copies["g", 4, 1, t].wait_recv()
+        gfull[z, t] = gp[z, t] + grecv[0, t, 3] + grecv[1, t, 3]
+    for s in range(1, 5):
+        for direction, t in FLOWS:
+            if s == 4 and direction != t:
+                continue
+            if s > 1:
+                copies["f", s - 1, direction, t].wait_recv()
+            q = (z + NZ - (s - 1)) % NZ if direction == 0 else (z + s - 1) % NZ
+            send(
+                ("f", s, direction, t), gfull.at[q, t], gfull.at[q, t],
+                gg_send.at[direction, t, s - 1], gg_recv.at[direction, t, s - 1],
+                up if direction == 0 else down,
+            )
+    for direction, t in FLOWS:
+        copies["f", 4 if direction == t else 3, direction, t].wait_recv()
+    for copy in copies.values():
+        copy.wait_send()
+    gram_ref[...] = gfull[...]
+
+
+def bond_and_gram(sources, environment, sites, extra, keep):
+    per_group, _, capacity, rows = environment.shape
+    vmem, anywhere = pl.BlockSpec(memory_space=pltpu.VMEM), pl.BlockSpec(memory_space=pl.ANY)
+    bf, f32 = jnp.bfloat16, jnp.float32
+    dma = pltpu.SemaphoreType.DMA
+    blocks = len(PAIRS)
+    return pl.pallas_call(
+        bond_kernel,
+        out_shape=(
+            jax.ShapeDtypeStruct(extra.shape, f32),
+            jax.ShapeDtypeStruct((NZ, 2, blocks, 16, T), f32),
+        ),
+        in_specs=[pl.BlockSpec(memory_space=pltpu.SMEM), anywhere, vmem, vmem, vmem],
+        out_specs=(vmem, vmem),
+        scratch_shapes=[pltpu.VMEM((64, ROWS, T), bf)] * CHUNKS
+        + [
+            pltpu.VMEM(environment.shape, bf),
+            pltpu.VMEM((CHUNKS, NZ, 2, ROWS, T), f32),
+            pltpu.VMEM((CHUNKS, 2, 2, 4, ROWS, T), bf),
+            pltpu.VMEM((CHUNKS, 2, 2, 4, ROWS, T), bf),
+            pltpu.VMEM((NZ, 2, blocks, 16, T), f32),
+            pltpu.VMEM((2, 2, 4, blocks, 16, T), f32),
+            pltpu.VMEM((2, 2, 4, blocks, 16, T), f32),
+            pltpu.VMEM((NZ, 2, blocks, 16, T), f32),
+            dma,
+            dma((CHUNKS, 2)),
+            dma((CHUNKS, 2, 12)),
+            dma((CHUNKS, 2, 12)),
+            dma((CHUNKS, 2, 2, 4)),
+            dma((CHUNKS, 2, 2, 4)),
+            dma((2, 2, 4)),
+            dma((2, 2, 4)),
+            dma((2, 2, 4)),
+            dma((2, 2, 4)),
+        ],
+        compiler_params=pltpu.CompilerParams(
+            vmem_limit_bytes=62 * 1024 * 1024, collective_id=0, has_side_effects=True
+        ),
+        name="bond",
+    )(sources, environment, sites, extra, keep)
+
+
 def lookup(values_table, indices):
     positions = jnp.arange(values_table.shape[0], dtype=jnp.int32)
     return jnp.sum(jnp.where(indices[..., None] == positions, values_table, 0), axis=-1)
@@ -179,21 +494,16 @@
     local_rows = row_index * rows_local + jnp.arange(rows_local, dtype=jnp.int32)
     keep_rows = (local_rows[None, :] < target_size[:, None])[:, :, None]
     site_kept = jnp.where(keep_rows, site_block, jnp.zeros((), site_block.dtype))
-    gathered = lax.all_gather(site_kept, "sector", axis=0, tiled=True)
-    picked = jnp.take(gathered, source_slots, axis=0)
-    partial_sum = jnp.einsum(
-        "ikcr,ikrw->icw", environment, picked, preferred_element_type=jnp.float32
-    ).astype(jnp.bfloat16)
-    summed = lax.psum_scatter(partial_sum, "row", scatter_dimension=1, tiled=True)
-    bond = summed.astype(jnp.float32) + chem_field[:, None, None] * site_kept.astype(jnp.float32)
-    bond = jnp.where(keep_rows, bond, 0.0)
-    part = jnp.einsum("iws,iwt->ist", bond, bond, precision=HI)
-    packed = jnp.stack(
-        [part[:, T * p : T * p + T, T * i : T * i + T] for p, i in PAIRS], axis=1
-    )
-    packed = lax.psum(packed, "row")
+    slots = source_slots
+    m, core = slots % 2, (slots // 2) % 2
+    x, y = (slots // 4) % SIDE, slots // (4 * SIDE)
+    sources = jnp.where(m == 0, (y * 2 + core) * SIDE + x, 32 + (x * 2 + core) * SIDE + y)
+    sites = jnp.transpose(site_kept.reshape(per_group, rows_local, CHUNKS, T), (2, 0, 1, 3))
+    extra = chem_field[:, None, None] * site_kept.astype(jnp.float32)
+    keep = jnp.broadcast_to(keep_rows.astype(jnp.float32), (per_group, rows_local, T))
+    bond, gram = bond_and_gram(sources, environment, sites, extra, keep)
     wide_root = jnp.broadcast_to(root[:, None, None], (per_group, 1, T))
-    iso, advanced = tail(packed, bond, next_site, wide_root)
+    iso, advanced = tail(gram, bond, next_site, wide_root)
     return (jnp.swapaxes(iso, 0, 1), advanced)
 
 

time: 299 us -> 191 us (0.64)
  waiting for transfers between devices: 210 us -> 0 us
  Pallas kernels: 41.8 us -> 175 us
  between operations: 13.9 us -> 0.69 us
  matrix products: 12.5 us -> 0 us
  local copies, waits for them, and re-layouts: 13.4 us -> 5.24 us
    pallas_call x0 -> x1, Pallas kernels: none -> 134 us  [bond_and_gram(): pl.pallas_call(bond_kernel, out_shape=(jax.ShapeDtypeStruct(extra.shape,...]
    all_gather x1 -> x0, waiting for transfers between devices: 78.7 us -> none  [local(): gathered = lax.all_gather(site_kept, 'sector', axis=0, tiled=True)]
    psum x1 -> x0, waiting for transfers between devices: 75.9 us -> none  [local(): packed = lax.psum(packed, 'row')]
    reduce_scatter x1 -> x0, waiting for transfers between devices: 55 us -> none  [local(): lax.psum_scatter(partial_sum, 'row', scatter_dimension=1, tiled=True)]
    dot_general x2 -> x0, matrix products: 12.5 us -> none  [the longest x1 10.6 us: local(): jnp.einsum('ikcr,ikrw->icw', environment, picked, preferred_element_type=...]
    gather x2 -> x0, local copies, waits for them, and re-layouts: 8.84 us -> none  [local(): picked = jnp.take(gathered, source_slots, axis=0)]
  transfers between devices with their start and end apart: 3 -> 0, of which waited for: 3 -> 0; matrix products, arithmetic and copies ran while one was open for 1% -> 0% of each run, Pallas kernels for 0% -> 0%
where the time goes in v2:
time: 191 us; the launch traced here: 190 us
  Pallas kernels  175 us (92%)
  other arithmetic  8.48 us (4%)
  local copies, waits for them, and re-layouts  5.24 us (3%)
    pallas_call x1, Pallas kernels, bond_and_gram(): pl.pallas_call(bond_kernel, out_shape=(jax.ShapeDtypeStruct(extra.shape,...  134 us
    pallas_call x1, Pallas kernels, tail(): pl.pallas_call(tail_kernel, out_shape=(jax.ShapeDtypeStruct((count, rows,...  41.8 us
    unnamed x7, local copies, waits for them, and re-layouts  4.32 us

profile of v2, /device:TPU:2, one launch (start us, length us, event | category | flops | bytes accessed | tf_op | source)
XLA Modules:
  0.0 189.8 jit_solution(5973149940709762380)
XLA Ops:
  0.6 0.0 copy-start.1
  0.7 0.9 fusion.1
  1.6 0.1 iota_compare_fusion.1
  1.7 0.8 select_reduce_fusion.1
  2.5 0.9 select_reduce_fusion
  3.4 0.6 compare_select_fusion.4.src_ref
  4.0 0.9 select_reduce_fusion.2
  4.9 0.1 broadcast_in_dim.105.root_ref
  4.9 0.1 fusion.4
  5.0 0.8 broadcast_in_dim.104.keep_ref
  5.9 2.0 %bitcast_bitcast_fusion.site_ref = bf16[4,2,256,128]{3,2,1,0:T(8,128)(2,1)} fusion(bf16[2,256,512]{2,1,0:T(8,128)(2,1)} %param.8, pred[2,256]{1,0:T(4,128)(4,1)S(1)} %get-tuple-element.17), kind=kLoop, calls=%fused_computation.1 | loop fusion | flops 262144 | bytes 1049088 | tf_op jit(solution)/shard_map/transpose | solution.py:501
  7.9 2.2 %convert_multiply_fusion.extra_ref = f32[2,256,512]{2,1,0:T(8,128)} fusion(f32[2]{0:T(128)S(1)} %get-tuple-element.19, bf16[2,256,512]{2,1,0:T(8,128)(2,1)} %param.8, pred[2,256]{1,0:T(4,128)(4,1)S(1)} %get-tuple-element.17), kind=kLoop, calls=%fused_computation | loop fusion | flops 786432 | bytes 1573384 | tf_op jit(solution)/shard_map/mul | solution.py:502
  10.1 133.6 %bond.1 = (f32[2,256,512]{2,1,0:T(8,128)}, f32[8,2,10,16,128]{4,3,2,1,0:T(8,128)}) custom-call(s32[2,4]{1,0:T(2,128)} %compare_select_fusion.4.src_ref, bf16[2,4,2048,256]{3,2,1,0:T(8,128)(2,1)} %env_ref.1, bf16[4,2,256,128]{3,2,1,0:T(8,128)(2,1)} %bitcast_bitcast_fusion.site_ref, f32[2,256,512]{2,1,0:T(8,128)} %convert_multiply_fusion.extra_ref, ...), custom_call_target="tpu_custom_call" | custom-call | tf_op jit(solution)/shard_map/bond/pallas_call | solution.py:437
  143.6 0.0 copy-done.1
  143.6 0.0 copy-start
  143.7 1.3 copy-done
  145.0 0.0 copy-start.2
  145.0 1.2 copy-done.2
  146.2 41.8 %tail.1 = (f32[2,256,512]{2,1,0:T(8,128)S(1)}, bf16[2,512,512]{2,1,0:T(8,128)(2,1)}) custom-call(f32[8,2,10,16,128]{4,3,2,1,0:T(8,128)S(1)} %copy-done, f32[2,256,512]{2,1,0:T(8,128)S(1)} %copy-done.2, bf16[2,512,512]{2,1,0:T(8,128)(2,1)S(1)} %copy-done.1, f32[2,1,128]{2,1,0:T(1,128)S(1)} %broadcast_in_dim.105.root_ref), custom_call_target="tpu_custom_call" | custom-call | tf_op jit(solution)/shard_map/tail/pallas_call | solution.py:140
  188.0 1.8 copy.13
  (3 shorter events, 0.0 us)
Async XLA Ops:
  0.6 143.0 %copy-start.1 = (bf16[2,512,512]{2,1,0:T(8,128)(2,1)S(1)}, bf16[2,512,512]{2,1,0:T(8,128)(2,1)}, u32[]{:S(2)}) copy-start(bf16[2,512,512]{2,1,0:T(8,128)(2,1)} %next_ref.1) | copy-start | bytes 3145732
  143.6 1.3 copy-start
  145.0 1.2 copy-start.2

commit v3 on v2

--- a/solution.py
+++ b/solution.py
@@ -7,9 +7,10 @@
 
 NB = 4
 T = 128
-GROUP = 4
+GROUP = 8
+HALF = 64
 HI = lax.Precision.HIGHEST
-PAIRS = [(p, i) for p in range(NB) for i in range(p, NB)]
+PAIRS = [(p, i) for i in range(NB) for p in range(i + 1)]
 
 
 def dot(a, b, dims, precision=HI):
@@ -18,20 +19,16 @@
     )
 
 
-def factor_tiles(a_tiles, u_ref, w_ref):
+def factor_tiles(a_tiles, r_ref):
     count = len(a_tiles)
-    rows8 = T // 8
+    rows8 = HALF // 8
     lane = lax.broadcasted_iota(jnp.int32, (8, T), 1)
     sub = lax.broadcasted_iota(jnp.int32, (8, T), 0)
-    w_tiles = [
-        [jnp.where(lane == sub + 8 * i, 1.0, 0.0).astype(jnp.float32) for i in range(rows8)]
-        for _ in range(count)
-    ]
 
     def spread(x, s):
         return jnp.broadcast_to(x[s : s + 1, :], (8, T))
 
-    for j0 in range(0, T, GROUP):
+    for j0 in range(0, HALF, GROUP):
         g = j0 // 8
         s0 = j0 - 8 * g
         state = []
@@ -44,40 +41,66 @@
                 for k in range(GROUP)
             ]
             rows = [spread(a_tiles[m][g], s0 + k) for k in range(GROUP)]
-            wrows = [spread(w_tiles[m][g], s0 + k) for k in range(GROUP)]
-            state.append((cols, rows, wrows))
+            state.append((cols, rows))
         for k in range(GROUP):
             for m in range(count):
-                cols, rows, wrows = state[m]
+                cols, rows = state[m]
                 rs = lax.rsqrt(spread(cols[k][0], s0 + k))
                 cols[k] = [c * rs for c in cols[k]]
                 rows[k] = rows[k] * rs
-                wrows[k] = wrows[k] * rs
                 for q in range(k + 1, GROUP):
                     f = spread(cols[k][0], s0 + q)
                     cols[q] = [c - l * f for c, l in zip(cols[q], cols[k])]
                     rows[q] = rows[q] - rows[k] * f
-                    wrows[q] = wrows[q] - wrows[k] * f
         for m in range(count):
-            cols, rows, wrows = state[m]
+            cols, rows = state[m]
             for k in range(GROUP):
                 j = j0 + k
-                keep = lane[:1] >= j
-                u_ref[m, j : j + 1, :] = jnp.where(keep, rows[k][:1], 0.0)
-                w_ref[m, j : j + 1, :] = wrows[k][:1]
+                r_ref[m, j : j + 1, :] = jnp.where(lane[:1] >= j, rows[k][:1], 0.0)
             last = s0 + GROUP == 8
             for i in range(g + 1 if last else g, rows8):
-                a, w = a_tiles[m][i], w_tiles[m][i]
+                a = a_tiles[m][i]
                 for k in range(GROUP):
                     l = cols[k][i - g]
                     if i == g:
                         l = jnp.where(sub >= s0 + GROUP, l, 0.0)
                     a = a - l * rows[k]
-                    w = w - l * wrows[k]
-                a_tiles[m][i], w_tiles[m][i] = a, w
-
-
-def tail_kernel(g_ref, b_ref, next_ref, root_ref, iso_ref, adv_ref, s_ref, d_ref, u_ref, w_ref):
+                a_tiles[m][i] = a
+
+
+def factor_block(a_list, u_ref, w_ref, r_ref):
+    lane = lax.broadcasted_iota(jnp.int32, (HALF, T), 1)
+    row = lax.broadcasted_iota(jnp.int32, (HALF, T), 0)
+    first = lane < HALF
+    eye = jnp.where(lane == row + HALF, 1.0, 0.0).astype(jnp.float32)
+
+    def turn(v):
+        return pltpu.roll(v, HALF, 1)
+
+    def tiles(v):
+        return [v[8 * i : 8 * i + 8] for i in range(HALF // 8)]
+
+    factor_tiles([tiles(jnp.where(first, a[:HALF], eye)) for a in a_list], r_ref)
+    kept, second = [], []
+    for m, a in enumerate(a_list):
+        r1 = r_ref[m]
+        w1 = turn(r1)
+        top = dot(w1[:, :HALF], a[:HALF], ((1,), (0,)))
+        rest = a[HALF:] - dot(top[:, HALF:], top, ((0,), (0,)))
+        kept.append((jnp.where(first, w1, 0.0), top))
+        second.append(tiles(jnp.where(first, turn(rest), eye)))
+        u_ref[m, :HALF] = jnp.where(first, r1, top)
+        w_ref[m, :HALF] = jnp.where(first, w1, 0.0)
+    factor_tiles(second, r_ref)
+    for m, (w1, top) in enumerate(kept):
+        r2 = r_ref[m]
+        w2 = turn(r2)
+        u_ref[m, HALF:] = jnp.where(first, 0.0, w2)
+        low = dot(top[:, HALF:], w1, ((0,), (0,)))
+        w_ref[m, HALF:] = jnp.where(first, -dot(w2[:, :HALF], low, ((1,), (0,))), r2)
+
+
+def tail_kernel(g_ref, b_ref, next_ref, root_ref, iso_ref, adv_ref, s_ref, d_ref, u_ref, w_ref, r_ref):
     count = b_ref.shape[0]
     eye = lax.broadcasted_iota(jnp.int32, (T, T), 0) == lax.broadcasted_iota(jnp.int32, (T, T), 1)
     scales = []
@@ -91,8 +114,7 @@
         scales.append(lax.rsqrt(jnp.full((1, T), trace / (NB * T) + 1e-6, jnp.float32)))
 
     def block(p, carry):
-        tiles = [[s_ref[m, p, p, 8 * i : 8 * i + 8, :] for i in range(T // 8)] for m in range(count)]
-        factor_tiles(tiles, u_ref, w_ref)
+        factor_block([s_ref[m, p, p] for m in range(count)], u_ref, w_ref, r_ref)
         for m in range(count):
             d_ref[m, p] = w_ref[m]
             s_ref[m, p, p] = u_ref[m]
@@ -124,7 +146,7 @@
                 x = x - dot(solved[i], s_ref[m, i, j], ((1,), (0,)))
             x = dot(x, d_ref[m, j], ((1,), (1,)))
             solved.append(x)
-            iso_ref[m, :, T * j : T * j + T] = x * root_ref[m]
+            iso_ref[m, :, T * j : T * j + T] = x * root_ref[m, :1, :]
         for p in range(NB):
             total = None
             for i in range(p, NB):
@@ -150,6 +172,7 @@
             pltpu.VMEM((count, NB, T, T), jnp.float32),
             pltpu.VMEM((count, T, T), jnp.float32),
             pltpu.VMEM((count, T, T), jnp.float32),
+            pltpu.VMEM((count, HALF, T), jnp.float32),
         ],
         compiler_params=pltpu.CompilerParams(vmem_limit_bytes=40 * 1024 * 1024),
         name="tail",
@@ -192,8 +215,8 @@
 
 
 def bond_kernel(
-    src_ref, env_ref, site_ref, extra_ref, keep_ref, bond_ref, gram_ref,
-    g0, g1, g2, g3, env_v, part, send_b, recv_b, gp, gsend, grecv, gfull,
+    owner_ref, pairs_ref, sizes_ref, charges_ref, env_ref, block_ref, bond_ref, gram_ref, root_ref,
+    g0, g1, g2, g3, site_ref, env_v, part, send_b, recv_b, gp, gsend, grecv, gfull,
     env_sem, own_sem, ag_send, ag_recv, rs_send, rs_recv, gr_send, gr_recv, gg_send, gg_recv,
 ):
     gath = (g0, g1, g2, g3)
@@ -216,8 +239,33 @@
         return 32 * m + ((maj % SIDE) * 2 + c) * SIDE + mino % SIDE
 
     barrier = pltpu.get_barrier_semaphore()
+    partners = [along(0, 0, 1), along(0, 0, 3), along(0, 1, 0), along(0, 3, 0), partner, up, down]
+    for device in partners:
+        pl.semaphore_signal(barrier, inc=1, device_id=device, device_id_type=MESH)
     env_copy = pltpu.make_async_copy(env_ref, env_v, env_sem)
     env_copy.start()
+    mine = [2 * sector, 2 * sector + 1]
+
+    def find(n, found):
+        return tuple(jnp.where(owner_ref[n] == slot_, n, f) for f, slot_ in zip(found, mine))
+
+    sectors = lax.fori_loop(0, 64, find, (jnp.int32(0), jnp.int32(0)))
+    limits, fields, source = [], [], []
+    for t in range(2):
+        limits.append(sizes_ref[sectors[t]] - z * ROWS)
+        fields.append(charges_ref[sectors[t]].astype(jnp.float32) * (2.0 / 64))
+        root_ref[t] = jnp.sqrt(jnp.full((8, T), sizes_ref[sectors[t]], jnp.int32).astype(jnp.float32))
+        for n in range(4):
+            place = owner_ref[pairs_ref[4 * sectors[t] + n]]
+            px, py, pc = (place // 4) % SIDE, place // (4 * SIDE), (place // 2) % 2
+            even = (py * 2 + pc) * SIDE + px
+            odd = 32 + (px * 2 + pc) * SIDE + py
+            source.append(jnp.where(place % 2 == 0, even, odd))
+    row_ids = lax.broadcasted_iota(jnp.int32, (ROWS, T), 0)
+    for j in range(CHUNKS):
+        for m in range(2):
+            value = block_ref[m, :, T * j : T * j + T].astype(jnp.float32)
+            site_ref[j, m] = jnp.where(row_ids < limits[m], value, 0.0).astype(jnp.bfloat16)
     own = []
     for j in range(CHUNKS):
         for m in range(2):
@@ -227,9 +275,6 @@
                 )
             )
             own[-1].start()
-    partners = [along(0, 0, 1), along(0, 0, 3), along(0, 1, 0), along(0, 3, 0), partner, up, down]
-    for device in partners:
-        pl.semaphore_signal(barrier, inc=1, device_id=device, device_id_type=MESH)
     pl.semaphore_wait(barrier, len(partners))
 
     copies = {}
@@ -302,7 +347,7 @@
             for k in range(4):
                 term = jnp.dot(
                     env_v[t, k, pl.ds(first, ROWS), :],
-                    gath[j][src_ref[t, k]],
+                    gath[j][jnp.where(t == 0, source[k], source[4 + k])],
                     preferred_element_type=jnp.float32,
                 )
                 total = term if total is None else total + term
@@ -331,17 +376,49 @@
         copies["r", j, 4, 0, t].wait_recv()
         copies["r", j, 4, 1, t].wait_recv()
         cols = pl.ds(T * j, T)
-        total = part[j, 0, t] + extra_ref[t, :, cols]
+        total = part[j, 0, t] + fields[t] * site_ref[j, t].astype(jnp.float32)
         total = total + recv_b[j, 0, t, 3].astype(jnp.float32) + recv_b[j, 1, t, 3].astype(jnp.float32)
-        bond_ref[t, :, cols] = jnp.where(keep_ref[t] > 0.5, total, 0.0)
+        bond_ref[t, :, cols] = jnp.where(row_ids < limits[t], total, 0.0)
 
     def grams(j):
         for t in range(2):
             for i in range(j + 1):
                 value = dot(bond_ref[t, :, T * i : T * i + T], bond_ref[t, :, T * j : T * j + T], ((0,), (0,)))
-                n = PAIRS.index((i, j))
                 for q in range(NZ):
-                    gp[q, t, n] = value[16 * q : 16 * q + 16]
+                    gp[j, q, t, i] = value[16 * q : 16 * q + 16]
+
+    def gram_hop(j, s, direction, t):
+        o = 5 - s if direction == 0 else 3 + s
+        value = gp[j, (z + o) % NZ, t, : j + 1]
+        if s > first_hop(direction, t):
+            copies["g", j, s - 1, direction, t].wait_recv()
+            value = value + grecv[j, direction, t, s - 2, : j + 1]
+        gsend[j, direction, t, s - 1, : j + 1] = value
+        send(
+            ("g", j, s, direction, t),
+            gsend.at[j, direction, t, s - 1, pl.ds(0, j + 1)],
+            grecv.at[j, direction, t, s - 1, pl.ds(0, j + 1)],
+            gr_send.at[j, direction, t, s - 1],
+            gr_recv.at[j, direction, t, s - 1],
+            up if direction == 0 else down,
+        )
+
+    def gram_sum(j, t):
+        copies["g", j, 4, 0, t].wait_recv()
+        copies["g", j, 4, 1, t].wait_recv()
+        total = gp[j, z, t, : j + 1] + grecv[j, 0, t, 3, : j + 1] + grecv[j, 1, t, 3, : j + 1]
+        gfull[z, t, j * (j + 1) // 2 : (j + 1) * (j + 2) // 2] = total
+
+    def gram_round(j, s, direction, t):
+        if s > 1:
+            copies["f", j, s - 1, direction, t].wait_recv()
+        q = (z + NZ - (s - 1)) % NZ if direction == 0 else (z + s - 1) % NZ
+        piece = gfull.at[q, t, pl.ds(j * (j + 1) // 2, j + 1)]
+        send(
+            ("f", j, s, direction, t), piece, piece,
+            gg_send.at[j, direction, t, s - 1], gg_recv.at[j, direction, t, s - 1],
+            up if direction == 0 else down,
+        )
 
     tasks = []
 
@@ -354,7 +431,8 @@
     for j in range(CHUNKS):
         ms = range(2)
         mins, majs = [axes(m)[0] for m in ms], [axes(m)[1] for m in ms]
-        task(("a1", j), lambda j=j: a1(j), 0.1, after=[("b1", j - 1)] if j else [],
+        task(("a1", j), lambda j=j: a1(j), 0.1,
+             after=[] if j == 0 else [("a2", 0)] if j == 1 else [("b1", j - 2)],
              sends=[((j, m, n), mins[m] + str(n), 64) for m in ms for n in (0, 1)])
         task(("a2", j), lambda j=j: a2(j), 0.1, needs=[(j, m, n) for m in ms for n in (0, 1)],
              sends=[((j, m, n + 2), mins[m] + str(n), 32) for m in ms for n in (0, 1)])
@@ -387,49 +465,35 @@
                  needs=[("r", j, 4, 0, t), ("r", j, 4, 1, t)], after=[("mm", j, 0)])
         task(("gram", j), lambda j=j: grams(j), 0.4 + 0.4 * j,
              after=[("finish", j, 0), ("finish", j, 1)] + ([("gram", j - 1)] if j else []))
+        for s in range(1, 5):
+            for direction, t in FLOWS:
+                if s >= first_hop(direction, t):
+                    more = s > first_hop(direction, t)
+                    task(("ghop", j, s, direction, t),
+                         lambda j=j, s=s, direction=direction, t=t: gram_hop(j, s, direction, t), 0.1,
+                         needs=[("g", j, s - 1, direction, t)] if more else [], after=[("gram", j)],
+                         sends=[(("g", j, s, direction, t), "z" + str(direction), 8 * (j + 1))])
+        for t in range(2):
+            task(("gsum", j, t), lambda j=j, t=t: gram_sum(j, t), 0.1,
+                 needs=[("g", j, 4, 0, t), ("g", j, 4, 1, t)], after=[("gram", j)])
+        for s in range(1, 5):
+            for direction, t in FLOWS:
+                if s < 4 or direction == t:
+                    task(("ground", j, s, direction, t),
+                         lambda j=j, s=s, direction=direction, t=t: gram_round(j, s, direction, t), 0.1,
+                         needs=[("f", j, s - 1, direction, t)] if s > 1 else [], after=[("gsum", j, t)],
+                         sends=[(("f", j, s, direction, t), "z" + str(direction), 8 * (j + 1))])
     for item in ordered(tasks):
         item["emit"]()
-
-    for s in range(1, 5):
+    for j in range(CHUNKS):
         for direction, t in FLOWS:
-            if s < first_hop(direction, t):
-                continue
-            o = 5 - s if direction == 0 else 3 + s
-            value = gp[(z + o) % NZ, t]
-            if s > first_hop(direction, t):
-                copies["g", s - 1, direction, t].wait_recv()
-                value = value + grecv[direction, t, s - 2]
-            gsend[direction, t, s - 1] = value
-            send(
-                ("g", s, direction, t), gsend.at[direction, t, s - 1], grecv.at[direction, t, s - 1],
-                gr_send.at[direction, t, s - 1], gr_recv.at[direction, t, s - 1],
-                up if direction == 0 else down,
-            )
-    for t in range(2):
-        copies["g", 4, 0, t].wait_recv()
-        copies["g", 4, 1, t].wait_recv()
-        gfull[z, t] = gp[z, t] + grecv[0, t, 3] + grecv[1, t, 3]
-    for s in range(1, 5):
-        for direction, t in FLOWS:
-            if s == 4 and direction != t:
-                continue
-            if s > 1:
-                copies["f", s - 1, direction, t].wait_recv()
-            q = (z + NZ - (s - 1)) % NZ if direction == 0 else (z + s - 1) % NZ
-            send(
-                ("f", s, direction, t), gfull.at[q, t], gfull.at[q, t],
-                gg_send.at[direction, t, s - 1], gg_recv.at[direction, t, s - 1],
-                up if direction == 0 else down,
-            )
-    for direction, t in FLOWS:
-        copies["f", 4 if direction == t else 3, direction, t].wait_recv()
+            copies["f", j, 4 if direction == t else 3, direction, t].wait_recv()
     for copy in copies.values():
         copy.wait_send()
     gram_ref[...] = gfull[...]
 
 
-def bond_and_gram(sources, environment, sites, extra, keep):
-    per_group, _, capacity, rows = environment.shape
+def bond_and_gram(owner, pairs, sizes, charges, environment, site_block):
     vmem, anywhere = pl.BlockSpec(memory_space=pltpu.VMEM), pl.BlockSpec(memory_space=pl.ANY)
     bf, f32 = jnp.bfloat16, jnp.float32
     dma = pltpu.SemaphoreType.DMA
@@ -437,20 +501,22 @@
     return pl.pallas_call(
         bond_kernel,
         out_shape=(
-            jax.ShapeDtypeStruct(extra.shape, f32),
+            jax.ShapeDtypeStruct(site_block.shape, f32),
             jax.ShapeDtypeStruct((NZ, 2, blocks, 16, T), f32),
+            jax.ShapeDtypeStruct((2, 8, T), f32),
         ),
-        in_specs=[pl.BlockSpec(memory_space=pltpu.SMEM), anywhere, vmem, vmem, vmem],
-        out_specs=(vmem, vmem),
+        in_specs=[pl.BlockSpec(memory_space=pltpu.SMEM)] * 4 + [anywhere, vmem],
+        out_specs=(vmem, vmem, vmem),
         scratch_shapes=[pltpu.VMEM((64, ROWS, T), bf)] * CHUNKS
         + [
+            pltpu.VMEM((CHUNKS, 2, ROWS, T), bf),
             pltpu.VMEM(environment.shape, bf),
             pltpu.VMEM((CHUNKS, NZ, 2, ROWS, T), f32),
             pltpu.VMEM((CHUNKS, 2, 2, 4, ROWS, T), bf),
             pltpu.VMEM((CHUNKS, 2, 2, 4, ROWS, T), bf),
-            pltpu.VMEM((NZ, 2, blocks, 16, T), f32),
-            pltpu.VMEM((2, 2, 4, blocks, 16, T), f32),
-            pltpu.VMEM((2, 2, 4, blocks, 16, T), f32),
+            pltpu.VMEM((CHUNKS, NZ, 2, NB, 16, T), f32),
+            pltpu.VMEM((CHUNKS, 2, 2, 4, NB, 16, T), f32),
+            pltpu.VMEM((CHUNKS, 2, 2, 4, NB, 16, T), f32),
             pltpu.VMEM((NZ, 2, blocks, 16, T), f32),
             dma,
             dma((CHUNKS, 2)),
@@ -458,52 +524,21 @@
             dma((CHUNKS, 2, 12)),
             dma((CHUNKS, 2, 2, 4)),
             dma((CHUNKS, 2, 2, 4)),
-            dma((2, 2, 4)),
-            dma((2, 2, 4)),
-            dma((2, 2, 4)),
-            dma((2, 2, 4)),
+            dma((CHUNKS, 2, 2, 4)),
+            dma((CHUNKS, 2, 2, 4)),
+            dma((CHUNKS, 2, 2, 4)),
+            dma((CHUNKS, 2, 2, 4)),
         ],
         compiler_params=pltpu.CompilerParams(
             vmem_limit_bytes=62 * 1024 * 1024, collective_id=0, has_side_effects=True
         ),
         name="bond",
-    )(sources, environment, sites, extra, keep)
-
-
-def lookup(values_table, indices):
-    positions = jnp.arange(values_table.shape[0], dtype=jnp.int32)
-    return jnp.sum(jnp.where(indices[..., None] == positions, values_table, 0), axis=-1)
+    )(owner, pairs, sizes, charges, environment, site_block)
 
 
 def local(environment, site_block, next_site, charges, sizes, pairs, owner):
-    per_group, rows_local, window = site_block.shape
-    sector_count = per_group * lax.axis_size("sector")
-    group_index = lax.axis_index("sector")
-    row_index = lax.axis_index("row")
-    sector_ids = jnp.arange(sector_count, dtype=jnp.int32)
-    my_slots = group_index * per_group + jnp.arange(per_group, dtype=jnp.int32)
-    my_sectors = jnp.sum(
-        jnp.where(owner[None, :] == my_slots[:, None], sector_ids[None, :], 0), axis=1
-    )
-    target_size = lookup(sizes, my_sectors)
-    chosen = (my_sectors[:, None] == sector_ids[None, :])[:, :, None]
-    source_sectors = jnp.sum(jnp.where(chosen, pairs[None, :, :], 0), axis=1)
-    source_slots = lookup(owner, source_sectors)
-    chem_field = 2.0 * lookup(charges, my_sectors).astype(jnp.float32) / sector_count
-    root = jnp.sqrt(target_size.astype(jnp.float32))
-    local_rows = row_index * rows_local + jnp.arange(rows_local, dtype=jnp.int32)
-    keep_rows = (local_rows[None, :] < target_size[:, None])[:, :, None]
-    site_kept = jnp.where(keep_rows, site_block, jnp.zeros((), site_block.dtype))
-    slots = source_slots
-    m, core = slots % 2, (slots // 2) % 2
-    x, y = (slots // 4) % SIDE, slots // (4 * SIDE)
-    sources = jnp.where(m == 0, (y * 2 + core) * SIDE + x, 32 + (x * 2 + core) * SIDE + y)
-    sites = jnp.transpose(site_kept.reshape(per_group, rows_local, CHUNKS, T), (2, 0, 1, 3))
-    extra = chem_field[:, None, None] * site_kept.astype(jnp.float32)
-    keep = jnp.broadcast_to(keep_rows.astype(jnp.float32), (per_group, rows_local, T))
-    bond, gram = bond_and_gram(sources, environment, sites, extra, keep)
-    wide_root = jnp.broadcast_to(root[:, None, None], (per_group, 1, T))
-    iso, advanced = tail(gram, bond, next_site, wide_root)
+    bond, gram, root = bond_and_gram(owner, pairs.reshape(-1), sizes, charges, environment, site_block)
+    iso, advanced = tail(gram, bond, next_site, root)
     return (jnp.swapaxes(iso, 0, 1), advanced)
 
 

time: 191 us -> 172 us (0.901)
  Pallas kernels: 175 us -> 162 us
  other arithmetic: 8.48 us -> 0 us
    pallas_call x1, Pallas kernels: 41.8 us -> 34.6 us  [tail(): pl.pallas_call(tail_kernel, out_shape=(jax.ShapeDtypeStruct((count, rows,...]
    pallas_call x1, Pallas kernels: 134 us -> 128 us  [bond_and_gram(): pl.pallas_call(bond_kernel, out_shape=(jax.ShapeDtypeStruct(site_block.sh...]
    reduce_sum x4 -> x0, other arithmetic: 3.5 us -> none  [the longest x2 1.75 us: lookup(): jnp.sum(jnp.where(indices[..., None] == positions, values_table, 0), axis...]
    mul x1 -> x0, other arithmetic: 2.19 us -> none  [local(): extra = chem_field[:, None, None] * site_kept.astype(jnp.float32)]
    transpose x1 -> x0, other arithmetic: 2.02 us -> none  [local(): jnp.transpose(site_kept.reshape(per_group, rows_local, CHUNKS, T), (2, 0,...]
    unnamed x7 -> x10, local copies, waits for them, and re-layouts: 4.32 us -> 5.87 us
where the time goes in v3:
time: 172 us; the launch traced here: 170 us
  Pallas kernels  162 us (94%)
  local copies, waits for them, and re-layouts  6.54 us (4%)
    pallas_call x1, Pallas kernels, bond_and_gram(): pl.pallas_call(bond_kernel, out_shape=(jax.ShapeDtypeStruct(site_block.sh...  128 us
    pallas_call x1, Pallas kernels, tail(): pl.pallas_call(tail_kernel, out_shape=(jax.ShapeDtypeStruct((count, rows,...  34.6 us
    unnamed x10, local copies, waits for them, and re-layouts  5.87 us

profile of v3, /device:TPU:2, one launch (start us, length us, event | category | flops | bytes accessed | tf_op | source)
XLA Modules:
  0.0 169.7 jit_solution(1962127969216414160)
XLA Ops:
  0.6 0.0 copy-start.1
  0.6 0.9 copy.10
  1.5 0.7 reshape.7.pairs_ref
  2.2 127.9 %bond.1 = (f32[2,256,512]{2,1,0:T(8,128)}, f32[8,2,10,16,128]{4,3,2,1,0:T(8,128)}, f32[2,8,128]{2,1,0:T(8,128)}) custom-call(s32[64]{0:T(128)} %owner_ref.1, s32[256]{0:T(256)} %reshape.7.pairs_ref, s32[64]{0:T(128)} %sizes_ref.1, s32[64]{0:T(128)} %charges_ref.1, bf16[2,4,2048,256]{3,2,1,0:T(8,128)(2,1)} %env_ref.1, bf16[2,256,512]{2,1,0:T(8,128)(2,1)} %block_ref.1), custom_call_target="tpu_custom_call" | custom-call | tf_op jit(solution)/shard_map/bond/pallas_call | solution.py:501
  130.1 0.0 copy-done.1
  130.1 0.0 copy-start
  130.1 1.3 copy-done
  131.4 0.0 copy-start.2
  131.4 1.2 copy-done.2
  132.7 0.0 copy-start.3
  132.7 0.7 copy-done.3
  133.4 34.6 %tail.1 = (f32[2,256,512]{2,1,0:T(8,128)S(1)}, bf16[2,512,512]{2,1,0:T(8,128)(2,1)}) custom-call(f32[8,2,10,16,128]{4,3,2,1,0:T(8,128)S(1)} %copy-done, f32[2,256,512]{2,1,0:T(8,128)S(1)} %copy-done.2, bf16[2,512,512]{2,1,0:T(8,128)(2,1)S(1)} %copy-done.1, f32[2,8,128]{2,1,0:T(8,128)S(1)} %copy-done.3), custom_call_target="tpu_custom_call" | custom-call | tf_op jit(solution)/shard_map/tail/pallas_call | solution.py:162
  167.9 1.8 %copy.11 = f32[256,2,512]{2,1,0:T(2,128)} copy(f32[256,2,512]{2,0,1:T(8,128)S(1)} %bitcast.1) | data formatting | bytes 2097152
Async XLA Ops:
  0.6 129.5 %copy-start.1 = (bf16[2,512,512]{2,1,0:T(8,128)(2,1)S(1)}, bf16[2,512,512]{2,1,0:T(8,128)(2,1)}, u32[]{:S(2)}) copy-start(bf16[2,512,512]{2,1,0:T(8,128)(2,1)} %next_ref.1) | copy-start | bytes 3145732
  130.1 1.3 copy-start
  131.4 1.2 copy-start.2
  132.7 0.7 copy-start.3

commit v4 on v3

--- a/solution.py
+++ b/solution.py
@@ -10,7 +10,6 @@
 GROUP = 8
 HALF = 64
 HI = lax.Precision.HIGHEST
-PAIRS = [(p, i) for i in range(NB) for p in range(i + 1)]
 
 
 def dot(a, b, dims, precision=HI):
@@ -68,7 +67,7 @@
                 a_tiles[m][i] = a
 
 
-def factor_block(a_list, u_ref, w_ref, r_ref):
+def factor_block(a_list, u_ref, w_ref, r_ref, between):
     lane = lax.broadcasted_iota(jnp.int32, (HALF, T), 1)
     row = lax.broadcasted_iota(jnp.int32, (HALF, T), 0)
     first = lane < HALF
@@ -91,6 +90,7 @@
         second.append(tiles(jnp.where(first, turn(rest), eye)))
         u_ref[m, :HALF] = jnp.where(first, r1, top)
         w_ref[m, :HALF] = jnp.where(first, w1, 0.0)
+    between()
     factor_tiles(second, r_ref)
     for m, (w1, top) in enumerate(kept):
         r2 = r_ref[m]
@@ -100,85 +100,6 @@
         w_ref[m, HALF:] = jnp.where(first, -dot(w2[:, :HALF], low, ((1,), (0,))), r2)
 
 
-def tail_kernel(g_ref, b_ref, next_ref, root_ref, iso_ref, adv_ref, s_ref, d_ref, u_ref, w_ref, r_ref):
-    count = b_ref.shape[0]
-    eye = lax.broadcasted_iota(jnp.int32, (T, T), 0) == lax.broadcasted_iota(jnp.int32, (T, T), 1)
-    scales = []
-    for m in range(count):
-        trace = jnp.zeros((), jnp.float32)
-        for n, (p, i) in enumerate(PAIRS):
-            for q in range(T // 16):
-                s_ref[m, p, i, 16 * q : 16 * q + 16, :] = g_ref[q, m, n]
-            if p == i:
-                trace = trace + jnp.sum(jnp.where(eye, s_ref[m, p, i], 0.0))
-        scales.append(lax.rsqrt(jnp.full((1, T), trace / (NB * T) + 1e-6, jnp.float32)))
-
-    def block(p, carry):
-        factor_block([s_ref[m, p, p] for m in range(count)], u_ref, w_ref, r_ref)
-        for m in range(count):
-            d_ref[m, p] = w_ref[m]
-            s_ref[m, p, p] = u_ref[m]
-
-        def panel(i, c):
-            for m in range(count):
-                s_ref[m, p, i] = dot(w_ref[m], s_ref[m, p, i], ((1,), (0,)))
-            return c
-
-        lax.fori_loop(p + 1, NB, panel, 0)
-
-        def trail(i, c):
-            def inner(k, c2):
-                for m in range(count):
-                    s_ref[m, i, k] = s_ref[m, i, k] - dot(s_ref[m, p, i], s_ref[m, p, k], ((0,), (0,)))
-                return c2
-
-            return lax.fori_loop(i, NB, inner, c)
-
-        lax.fori_loop(p + 1, NB, trail, 0)
-        return carry
-
-    lax.fori_loop(0, NB, block, 0)
-    for m in range(count):
-        solved = []
-        for j in range(NB):
-            x = b_ref[m, :, T * j : T * j + T]
-            for i in range(j):
-                x = x - dot(solved[i], s_ref[m, i, j], ((1,), (0,)))
-            x = dot(x, d_ref[m, j], ((1,), (1,)))
-            solved.append(x)
-            iso_ref[m, :, T * j : T * j + T] = x * root_ref[m, :1, :]
-        for p in range(NB):
-            total = None
-            for i in range(p, NB):
-                up = (s_ref[m, p, i] * scales[m]).astype(jnp.bfloat16)
-                term = dot(up, next_ref[m, T * i : T * i + T, :], ((1,), (0,)), None)
-                total = term if total is None else total + term
-            adv_ref[m, T * p : T * p + T, :] = total.astype(jnp.bfloat16)
-
-
-def tail(gram, bond, next_site, root):
-    count, rows, window = bond.shape
-    vmem = pl.BlockSpec(memory_space=pltpu.VMEM)
-    return pl.pallas_call(
-        tail_kernel,
-        out_shape=(
-            jax.ShapeDtypeStruct((count, rows, window), jnp.float32),
-            jax.ShapeDtypeStruct(next_site.shape, jnp.bfloat16),
-        ),
-        in_specs=[vmem] * 4,
-        out_specs=(vmem, vmem),
-        scratch_shapes=[
-            pltpu.VMEM((count, NB, NB, T, T), jnp.float32),
-            pltpu.VMEM((count, NB, T, T), jnp.float32),
-            pltpu.VMEM((count, T, T), jnp.float32),
-            pltpu.VMEM((count, T, T), jnp.float32),
-            pltpu.VMEM((count, HALF, T), jnp.float32),
-        ],
-        compiler_params=pltpu.CompilerParams(vmem_limit_bytes=40 * 1024 * 1024),
-        name="tail",
-    )(gram, bond, next_site, root)
-
-
 CHUNKS = 4
 NZ = 8
 SIDE = 4
@@ -192,7 +113,7 @@
 
 
 def ordered(tasks):
-    rate = {"x": 47.0, "y": 47.0, "z": 47.0, "c": 300.0}
+    rate = {"x": 43.0, "y": 43.0, "z": 43.0, "c": 300.0}
     link_free, arrival, done, order = {}, {}, set(), []
     now, left = 0.0, list(tasks)
     while left:
@@ -215,9 +136,10 @@
 
 
 def bond_kernel(
-    owner_ref, pairs_ref, sizes_ref, charges_ref, env_ref, block_ref, bond_ref, gram_ref, root_ref,
+    owner_ref, pairs_ref, sizes_ref, charges_ref, env_ref, block_ref, next_hbm, iso_ref, adv_ref,
     g0, g1, g2, g3, site_ref, env_v, part, send_b, recv_b, gp, gsend, grecv, gfull,
-    env_sem, own_sem, ag_send, ag_recv, rs_send, rs_recv, gr_send, gr_recv, gg_send, gg_recv,
+    bond_ref, root_ref, next_ref, s_ref, d_ref, u_ref, w_ref, r_ref,
+    env_sem, next_sem, own_sem, ag_send, ag_recv, rs_send, rs_recv, gr_send, gr_recv, gg_send, gg_recv,
 ):
     gath = (g0, g1, g2, g3)
     sector, z = lax.axis_index("sector"), lax.axis_index("row")
@@ -244,6 +166,8 @@
         pl.semaphore_signal(barrier, inc=1, device_id=device, device_id_type=MESH)
     env_copy = pltpu.make_async_copy(env_ref, env_v, env_sem)
     env_copy.start()
+    next_copy = pltpu.make_async_copy(next_hbm, next_ref, next_sem)
+    next_copy.start()
     mine = [2 * sector, 2 * sector + 1]
 
     def find(n, found):
@@ -279,12 +203,13 @@
 
     copies = {}
 
-    def send(key, src, dst, ssem, rsem, device):
+    def send(key, src, dst, ssem, rsem, device, late=False):
         copy = pltpu.make_async_remote_copy(
             src_ref=src, dst_ref=dst, send_sem=ssem, recv_sem=rsem, device_id=device, device_id_type=MESH
         )
-        copy.start()
         copies[key] = copy
+        if not late:
+            copy.start()
 
     def ag_send_one(j, m, n, ref, device, src=None):
         send((j, m, n), ref if src is None else src, ref, ag_send.at[j, m, n], ag_recv.at[j, m, n], device)
@@ -387,6 +312,28 @@
                 for q in range(NZ):
                     gp[j, q, t, i] = value[16 * q : 16 * q + 16]
 
+    for j in range(CHUNKS):
+        for s in range(1, 5):
+            for direction, t in FLOWS:
+                device = up if direction == 0 else down
+                if s >= first_hop(direction, t):
+                    send(
+                        ("g", j, s, direction, t),
+                        gsend.at[j, direction, t, s - 1, pl.ds(0, j + 1)],
+                        grecv.at[j, direction, t, s - 1, pl.ds(0, j + 1)],
+                        gr_send.at[j, direction, t, s - 1],
+                        gr_recv.at[j, direction, t, s - 1],
+                        device, late=True,
+                    )
+                if s < 4 or direction == t:
+                    q = (z + NZ - (s - 1)) % NZ if direction == 0 else (z + s - 1) % NZ
+                    piece = gfull.at[q, t, pl.ds(j * (j + 1) // 2, j + 1)]
+                    send(
+                        ("f", j, s, direction, t), piece, piece,
+                        gg_send.at[j, direction, t, s - 1], gg_recv.at[j, direction, t, s - 1],
+                        device, late=True,
+                    )
+
     def gram_hop(j, s, direction, t):
         o = 5 - s if direction == 0 else 3 + s
         value = gp[j, (z + o) % NZ, t, : j + 1]
@@ -394,14 +341,7 @@
             copies["g", j, s - 1, direction, t].wait_recv()
             value = value + grecv[j, direction, t, s - 2, : j + 1]
         gsend[j, direction, t, s - 1, : j + 1] = value
-        send(
-            ("g", j, s, direction, t),
-            gsend.at[j, direction, t, s - 1, pl.ds(0, j + 1)],
-            grecv.at[j, direction, t, s - 1, pl.ds(0, j + 1)],
-            gr_send.at[j, direction, t, s - 1],
-            gr_recv.at[j, direction, t, s - 1],
-            up if direction == 0 else down,
-        )
+        copies["g", j, s, direction, t].start()
 
     def gram_sum(j, t):
         copies["g", j, 4, 0, t].wait_recv()
@@ -412,13 +352,49 @@
     def gram_round(j, s, direction, t):
         if s > 1:
             copies["f", j, s - 1, direction, t].wait_recv()
-        q = (z + NZ - (s - 1)) % NZ if direction == 0 else (z + s - 1) % NZ
-        piece = gfull.at[q, t, pl.ds(j * (j + 1) // 2, j + 1)]
-        send(
-            ("f", j, s, direction, t), piece, piece,
-            gg_send.at[j, direction, t, s - 1], gg_recv.at[j, direction, t, s - 1],
-            up if direction == 0 else down,
-        )
+        copies["f", j, s, direction, t].start()
+
+    def hops(j, s):
+        for direction, t in FLOWS:
+            if s >= first_hop(direction, t):
+                gram_hop(j, s, direction, t)
+
+    def sums(j):
+        for t in range(2):
+            gram_sum(j, t)
+
+    def rounds(j, s):
+        for direction, t in FLOWS:
+            if s < 4 or direction == t:
+                gram_round(j, s, direction, t)
+
+    def last(j):
+        for direction, t in FLOWS:
+            copies["f", j, 4 if direction == t else 3, direction, t].wait_recv()
+        for i in range(j + 1):
+            for m in range(2):
+                for q in range(NZ):
+                    s_ref[m, i, j, 16 * q : 16 * q + 16, :] = gfull[q, m, j * (j + 1) // 2 + i]
+
+    late_steps = {
+        (0, 0): lambda: (last(0), hops(3, 1)),
+        (0, 1): lambda: (sums(2), rounds(2, 1), hops(3, 2)),
+        (0, 2): lambda: (rounds(2, 2), hops(3, 3)),
+        (1, 0): lambda: (last(1), rounds(2, 3), hops(3, 4)),
+        (1, 1): lambda: (rounds(2, 4), sums(3), rounds(3, 1)),
+        (1, 2): lambda: rounds(3, 2),
+        (2, 0): lambda: (last(2), rounds(3, 3)),
+        (2, 1): lambda: rounds(3, 4),
+        (3, 0): lambda: last(3),
+    }
+
+    def point(p, n):
+        for (block, place), run in late_steps.items():
+            if place == n:
+
+                @pl.when(p == block)
+                def _(run=run):
+                    run()
 
     tasks = []
 
@@ -467,46 +443,90 @@
              after=[("finish", j, 0), ("finish", j, 1)] + ([("gram", j - 1)] if j else []))
         for s in range(1, 5):
             for direction, t in FLOWS:
-                if s >= first_hop(direction, t):
+                if s >= first_hop(direction, t) and j < 3:
                     more = s > first_hop(direction, t)
                     task(("ghop", j, s, direction, t),
                          lambda j=j, s=s, direction=direction, t=t: gram_hop(j, s, direction, t), 0.1,
                          needs=[("g", j, s - 1, direction, t)] if more else [], after=[("gram", j)],
                          sends=[(("g", j, s, direction, t), "z" + str(direction), 8 * (j + 1))])
-        for t in range(2):
+        for t in range(2 if j < 2 else 0):
             task(("gsum", j, t), lambda j=j, t=t: gram_sum(j, t), 0.1,
                  needs=[("g", j, 4, 0, t), ("g", j, 4, 1, t)], after=[("gram", j)])
         for s in range(1, 5):
             for direction, t in FLOWS:
-                if s < 4 or direction == t:
+                if j < 2 and (s < 4 or direction == t):
                     task(("ground", j, s, direction, t),
                          lambda j=j, s=s, direction=direction, t=t: gram_round(j, s, direction, t), 0.1,
                          needs=[("f", j, s - 1, direction, t)] if s > 1 else [], after=[("gsum", j, t)],
                          sends=[(("f", j, s, direction, t), "z" + str(direction), 8 * (j + 1))])
     for item in ordered(tasks):
         item["emit"]()
-    for j in range(CHUNKS):
-        for direction, t in FLOWS:
-            copies["f", j, 4 if direction == t else 3, direction, t].wait_recv()
+
+    def block(p, carry):
+        point(p, 0)
+        def column(i, c):
+            def above(k, c2):
+                for m in range(2):
+                    s_ref[m, i, p] = s_ref[m, i, p] - dot(s_ref[m, k, i], s_ref[m, k, p], ((0,), (0,)))
+                return c2
+
+            lax.fori_loop(0, i, above, 0)
+            for m in range(2):
+                value = dot(d_ref[m, i], s_ref[m, i, p], ((1,), (0,)))
+                s_ref[m, i, p] = value
+                s_ref[m, p, p] = s_ref[m, p, p] - dot(value, value, ((0,), (0,)))
+            return c
+
+        lax.fori_loop(0, p, column, 0)
+        factor_block([s_ref[m, p, p] for m in range(2)], u_ref, w_ref, r_ref, lambda: point(p, 1))
+        for m in range(2):
+            d_ref[m, p] = w_ref[m]
+            s_ref[m, p, p] = u_ref[m]
+        point(p, 2)
+        return carry
+
+    lax.fori_loop(0, NB, block, 0)
+    next_copy.wait()
+    row16 = lax.broadcasted_iota(jnp.int32, (16, T), 0)
+    lane16 = lax.broadcasted_iota(jnp.int32, (16, T), 1)
+    for m in range(2):
+        trace = jnp.zeros((16, T), jnp.float32)
+        for p in range(NB):
+            for q in range(NZ):
+                trace = trace + jnp.where(lane16 == row16 + 16 * q, gfull[q, m, p * (p + 3) // 2], 0.0)
+        scale = lax.rsqrt(jnp.full((1, T), jnp.sum(trace) / (NB * T) + 1e-6, jnp.float32))
+        solved = []
+        for j in range(NB):
+            value = bond_ref[m, :, T * j : T * j + T]
+            for i in range(j):
+                value = value - dot(solved[i], s_ref[m, i, j], ((1,), (0,)))
+            value = dot(value, d_ref[m, j], ((1,), (1,)))
+            solved.append(value)
+            iso_ref[m, :, T * j : T * j + T] = value * root_ref[m, :1, :]
+        for p in range(NB):
+            total = None
+            for i in range(p, NB):
+                up_block = (s_ref[m, p, i] * scale).astype(jnp.bfloat16)
+                term = dot(up_block, next_ref[m, T * i : T * i + T, :], ((1,), (0,)), None)
+                total = term if total is None else total + term
+            adv_ref[m, T * p : T * p + T, :] = total.astype(jnp.bfloat16)
     for copy in copies.values():
         copy.wait_send()
-    gram_ref[...] = gfull[...]
-
-
-def bond_and_gram(owner, pairs, sizes, charges, environment, site_block):
+
+
+def site_step(owner, pairs, sizes, charges, environment, site_block, next_site):
     vmem, anywhere = pl.BlockSpec(memory_space=pltpu.VMEM), pl.BlockSpec(memory_space=pl.ANY)
     bf, f32 = jnp.bfloat16, jnp.float32
     dma = pltpu.SemaphoreType.DMA
-    blocks = len(PAIRS)
+    blocks = NB * (NB + 1) // 2
     return pl.pallas_call(
         bond_kernel,
         out_shape=(
             jax.ShapeDtypeStruct(site_block.shape, f32),
-            jax.ShapeDtypeStruct((NZ, 2, blocks, 16, T), f32),
-            jax.ShapeDtypeStruct((2, 8, T), f32),
+            jax.ShapeDtypeStruct(next_site.shape, bf),
         ),
-        in_specs=[pl.BlockSpec(memory_space=pltpu.SMEM)] * 4 + [anywhere, vmem],
-        out_specs=(vmem, vmem, vmem),
+        in_specs=[pl.BlockSpec(memory_space=pltpu.SMEM)] * 4 + [anywhere, vmem, anywhere],
+        out_specs=(vmem, vmem),
         scratch_shapes=[pltpu.VMEM((64, ROWS, T), bf)] * CHUNKS
         + [
             pltpu.VMEM((CHUNKS, 2, ROWS, T), bf),
@@ -518,6 +538,15 @@
             pltpu.VMEM((CHUNKS, 2, 2, 4, NB, 16, T), f32),
             pltpu.VMEM((CHUNKS, 2, 2, 4, NB, 16, T), f32),
             pltpu.VMEM((NZ, 2, blocks, 16, T), f32),
+            pltpu.VMEM(site_block.shape, f32),
+            pltpu.VMEM((2, 8, T), f32),
+            pltpu.VMEM(next_site.shape, bf),
+            pltpu.VMEM((2, NB, NB, T, T), f32),
+            pltpu.VMEM((2, NB, T, T), f32),
+            pltpu.VMEM((2, T, T), f32),
+            pltpu.VMEM((2, T, T), f32),
+            pltpu.VMEM((2, HALF, T), f32),
+            dma,
             dma,
             dma((CHUNKS, 2)),
             dma((CHUNKS, 2, 12)),
@@ -530,15 +559,16 @@
             dma((CHUNKS, 2, 2, 4)),
         ],
         compiler_params=pltpu.CompilerParams(
-            vmem_limit_bytes=62 * 1024 * 1024, collective_id=0, has_side_effects=True
+            vmem_limit_bytes=63 * 1024 * 1024, collective_id=0, has_side_effects=True
         ),
         name="bond",
-    )(owner, pairs, sizes, charges, environment, site_block)
+    )(owner, pairs, sizes, charges, environment, site_block, next_site)
 
 
 def local(environment, site_block, next_site, charges, sizes, pairs, owner):
-    bond, gram, root = bond_and_gram(owner, pairs.reshape(-1), sizes, charges, environment, site_block)
-    iso, advanced = tail(gram, bond, next_site, root)
+    iso, advanced = site_step(
+        owner, pairs.reshape(-1), sizes, charges, environment, site_block, next_site
+    )
     return (jnp.swapaxes(iso, 0, 1), advanced)
 
 

time: 172 us -> 155 us (0.901)
  Pallas kernels: 162 us -> 147 us
    pallas_call x2 -> x1, Pallas kernels: 162 us -> 147 us  [site_step(): pl.pallas_call(bond_kernel, out_shape=(jax.ShapeDtypeStruct(site_block.sh...]
    unnamed x10 -> x3, local copies, waits for them, and re-layouts: 5.87 us -> 6.04 us
where the time goes in v4:
time: 155 us; the launch traced here: 154 us
  Pallas kernels  147 us (95%)
  local copies, waits for them, and re-layouts  6.71 us (4%)
    pallas_call x1, Pallas kernels, site_step(): pl.pallas_call(bond_kernel, out_shape=(jax.ShapeDtypeStruct(site_block.sh...  147 us
    unnamed x3, local copies, waits for them, and re-layouts  6.04 us

profile of v4, /device:TPU:2, one launch (start us, length us, event | category | flops | bytes accessed | tf_op | source)
XLA Modules:
  0.0 154.1 jit_solution(3557955779722563672)
XLA Ops:
  0.6 0.8 copy.10
  1.4 0.7 reshape.7.pairs_ref
  2.1 146.8 %bond.1 = (f32[2,256,512]{2,1,0:T(8,128)}, bf16[2,512,512]{2,1,0:T(8,128)(2,1)}) custom-call(s32[64]{0:T(128)} %owner_ref.1, s32[256]{0:T(256)} %reshape.7.pairs_ref, s32[64]{0:T(128)} %sizes_ref.1, s32[64]{0:T(128)} %charges_ref.1, bf16[2,4,2048,256]{3,2,1,0:T(8,128)(2,1)} %env_ref.1, bf16[2,256,512]{2,1,0:T(8,128)(2,1)} %block_ref.1, ...), custom_call_target="tpu_custom_call" | custom-call | tf_op jit(solution)/shard_map/bond/pallas_call | solution.py:522
  148.8 3.0 %copy.11 = f32[256,2,512]{2,1,0:T(2,128)} copy(f32[256,2,512]{2,0,1:T(8,128)} %bitcast.1) | data formatting | bytes 2097152
  151.8 2.3 %copy.13 = bf16[2,512,512]{2,1,0:T(8,128)(2,1)} copy(bf16[2,512,512]{2,1,0:T(8,128)(2,1)} %get-tuple-element.13) | data formatting | bytes 2097152

commit v5 on v4

--- a/solution.py
+++ b/solution.py
@@ -237,8 +237,10 @@
             own[2 * j + m].wait()
             copies[j, m, 2].wait_recv()
             copies[j, m, 3].wait_recv()
-            ag_send_one(j, m, 4, group(j, m, 0), along(m, 1, 0))
-            ag_send_one(j, m, 5, group(j, m, 0), along(m, 3, 0))
+            ag_send_one(j, m, 4, group(j, m, 0, 0, 2), along(m, 1, 0))
+            ag_send_one(j, m, 5, group(j, m, 0, 2, 2), along(m, 3, 0))
+            ag_send_one(j, m, 12, group(j, m, 0, 2, 2), along(m, 1, 0))
+            ag_send_one(j, m, 13, group(j, m, 0, 0, 2), along(m, 3, 0))
             ag_send_one(j, m, 8, group(j, m, 0), partner)
 
     def b2(j):
@@ -247,6 +249,11 @@
             ag_send_one(j, m, 6, group(j, m, 3, 0, 2), along(m, 1, 0))
             copies[j, m, 5].wait_recv()
             ag_send_one(j, m, 7, group(j, m, 1, 2, 2), along(m, 3, 0))
+
+    def b2c(j):
+        for m in range(2):
+            copies[j, m, 12].wait_recv()
+            copies[j, m, 13].wait_recv()
             ag_send_one(j, m, 9, group(j, m, 3), partner)
             ag_send_one(j, m, 10, group(j, m, 1), partner)
 
@@ -377,11 +384,11 @@
                     s_ref[m, i, j, 16 * q : 16 * q + 16, :] = gfull[q, m, j * (j + 1) // 2 + i]
 
     late_steps = {
-        (0, 0): lambda: (last(0), hops(3, 1)),
-        (0, 1): lambda: (sums(2), rounds(2, 1), hops(3, 2)),
-        (0, 2): lambda: (rounds(2, 2), hops(3, 3)),
-        (1, 0): lambda: (last(1), rounds(2, 3), hops(3, 4)),
-        (1, 1): lambda: (rounds(2, 4), sums(3), rounds(3, 1)),
+        (0, 0): lambda: (last(0), hops(3, 1), sums(2), rounds(2, 1)),
+        (0, 1): lambda: (hops(3, 2), rounds(2, 2)),
+        (0, 2): lambda: (hops(3, 3), rounds(2, 3)),
+        (1, 0): lambda: (last(1), hops(3, 4), rounds(2, 4)),
+        (1, 1): lambda: (sums(3), rounds(3, 1)),
         (1, 2): lambda: rounds(3, 2),
         (2, 0): lambda: (last(2), rounds(3, 3)),
         (2, 1): lambda: rounds(3, 4),
@@ -408,18 +415,19 @@
         ms = range(2)
         mins, majs = [axes(m)[0] for m in ms], [axes(m)[1] for m in ms]
         task(("a1", j), lambda j=j: a1(j), 0.1,
-             after=[] if j == 0 else [("a2", 0)] if j == 1 else [("b1", j - 2)],
+             after=[[], [("a1", 0)], [("a2", 0)], [("b1", 1)]][j],
              sends=[((j, m, n), mins[m] + str(n), 64) for m in ms for n in (0, 1)])
         task(("a2", j), lambda j=j: a2(j), 0.1, needs=[(j, m, n) for m in ms for n in (0, 1)],
              sends=[((j, m, n + 2), mins[m] + str(n), 32) for m in ms for n in (0, 1)])
         task(("b1", j), lambda j=j: b1(j), 0.1, needs=[(j, m, n) for m in ms for n in (2, 3)],
              after=[("b2", j - 1)] if j else [],
-             sends=[((j, m, n + 4), majs[m] + str(n), 256) for m in ms for n in (0, 1)]
+             sends=[((j, m, n + 4 + late), majs[m] + str(n), 128) for m in ms for late in (0, 8) for n in (0, 1)]
              + [((j, m, 8), "c", 256) for m in ms])
         task(("b2", j), lambda j=j: b2(j), 0.1, needs=[(j, m, n) for m in ms for n in (4, 5)],
-             sends=[((j, m, n + 6), majs[m] + str(n), 128) for m in ms for n in (0, 1)]
-             + [((j, m, n), "c", 256) for m in ms for n in (9, 10)])
-        task(("b3", j), lambda j=j: b3(j), 0.1, needs=[(j, m, n) for m in ms for n in (6, 7)],
+             sends=[((j, m, n + 6), majs[m] + str(n), 128) for m in ms for n in (0, 1)])
+        task(("b2c", j), lambda j=j: b2c(j), 0.1, needs=[(j, m, n) for m in ms for n in (12, 13)],
+             after=[("b2", j)], sends=[((j, m, n), "c", 256) for m in ms for n in (9, 10)])
+        task(("b3", j), lambda j=j: b3(j), 0.1, needs=[(j, m, n) for m in ms for n in (6, 7)], after=[("b2c", j)],
              sends=[((j, m, 11), "c", 256) for m in ms])
         task(("ready", j), lambda j=j: ready(j), 0.1, needs=[(j, m, n) for m in ms for n in (8, 9, 10, 11)])
         before = ("ready", j)
@@ -549,8 +557,8 @@
             dma,
             dma,
             dma((CHUNKS, 2)),
-            dma((CHUNKS, 2, 12)),
-            dma((CHUNKS, 2, 12)),
+            dma((CHUNKS, 2, 14)),
+            dma((CHUNKS, 2, 14)),
             dma((CHUNKS, 2, 2, 4)),
             dma((CHUNKS, 2, 2, 4)),
             dma((CHUNKS, 2, 2, 4)),

time: 155 us -> 153 us (0.987)
  no operation moved by 1% of the time
where the time goes in v5:
time: 153 us
  Pallas kernels  146 us (95%)
  local copies, waits for them, and re-layouts  6.71 us (4%)
    pallas_call x1, Pallas kernels, site_step(): pl.pallas_call(bond_kernel, out_shape=(jax.ShapeDtypeStruct(site_block.sh...  146 us
    unnamed x3, local copies, waits for them, and re-layouts  6.04 us

profile of v5, /device:TPU:2, one launch (start us, length us, event | category | flops | bytes accessed | tf_op | source)
XLA Modules:
  0.0 153.2 jit_solution(10393603601957144436)
XLA Ops:
  0.6 0.8 copy.10
  1.4 0.7 reshape.7.pairs_ref
  2.1 145.8 %bond.1 = (f32[2,256,512]{2,1,0:T(8,128)}, bf16[2,512,512]{2,1,0:T(8,128)(2,1)}) custom-call(s32[64]{0:T(128)} %owner_ref.1, s32[256]{0:T(256)} %reshape.7.pairs_ref, s32[64]{0:T(128)} %sizes_ref.1, s32[64]{0:T(128)} %charges_ref.1, bf16[2,4,2048,256]{3,2,1,0:T(8,128)(2,1)} %env_ref.1, bf16[2,256,512]{2,1,0:T(8,128)(2,1)} %block_ref.1, ...), custom_call_target="tpu_custom_call" | custom-call | tf_op jit(solution)/shard_map/bond/pallas_call | solution.py:530
  147.9 3.0 %copy.11 = f32[256,2,512]{2,1,0:T(2,128)} copy(f32[256,2,512]{2,0,1:T(8,128)} %bitcast.1) | data formatting | bytes 2097152
  150.9 2.3 %copy.13 = bf16[2,512,512]{2,1,0:T(8,128)(2,1)} copy(bf16[2,512,512]{2,1,0:T(8,128)(2,1)} %get-tuple-element.13) | data formatting | bytes 2097152

commit v6 on v5

--- a/solution.py
+++ b/solution.py
@@ -18,7 +18,7 @@
     )
 
 
-def factor_tiles(a_tiles, r_ref):
+def factor_tiles(a_tiles, r_ref, inside=None):
     count = len(a_tiles)
     rows8 = HALF // 8
     lane = lax.broadcasted_iota(jnp.int32, (8, T), 1)
@@ -28,6 +28,8 @@
         return jnp.broadcast_to(x[s : s + 1, :], (8, T))
 
     for j0 in range(0, HALF, GROUP):
+        if inside is not None and j0 == 6 * GROUP:
+            inside()
         g = j0 // 8
         s0 = j0 - 8 * g
         state = []
@@ -67,7 +69,7 @@
                 a_tiles[m][i] = a
 
 
-def factor_block(a_list, u_ref, w_ref, r_ref, between):
+def factor_block(a_list, u_ref, w_ref, r_ref, between, inside):
     lane = lax.broadcasted_iota(jnp.int32, (HALF, T), 1)
     row = lax.broadcasted_iota(jnp.int32, (HALF, T), 0)
     first = lane < HALF
@@ -91,7 +93,7 @@
         u_ref[m, :HALF] = jnp.where(first, r1, top)
         w_ref[m, :HALF] = jnp.where(first, w1, 0.0)
     between()
-    factor_tiles(second, r_ref)
+    factor_tiles(second, r_ref, inside)
     for m, (w1, top) in enumerate(kept):
         r2 = r_ref[m]
         w2 = turn(r2)
@@ -385,13 +387,15 @@
 
     late_steps = {
         (0, 0): lambda: (last(0), hops(3, 1), sums(2), rounds(2, 1)),
-        (0, 1): lambda: (hops(3, 2), rounds(2, 2)),
-        (0, 2): lambda: (hops(3, 3), rounds(2, 3)),
-        (1, 0): lambda: (last(1), hops(3, 4), rounds(2, 4)),
-        (1, 1): lambda: (sums(3), rounds(3, 1)),
-        (1, 2): lambda: rounds(3, 2),
-        (2, 0): lambda: (last(2), rounds(3, 3)),
-        (2, 1): lambda: rounds(3, 4),
+        (0, 2): lambda: (hops(3, 2), rounds(2, 2)),
+        (0, 3): lambda: (hops(3, 3), rounds(2, 3)),
+        (1, 0): lambda: last(1),
+        (1, 1): lambda: (hops(3, 4), rounds(2, 4)),
+        (1, 2): lambda: (sums(3), rounds(3, 1)),
+        (1, 3): lambda: rounds(3, 2),
+        (2, 0): lambda: last(2),
+        (2, 1): lambda: rounds(3, 3),
+        (2, 2): lambda: rounds(3, 4),
         (3, 0): lambda: last(3),
     }
 
@@ -486,11 +490,28 @@
             return c
 
         lax.fori_loop(0, p, column, 0)
-        factor_block([s_ref[m, p, p] for m in range(2)], u_ref, w_ref, r_ref, lambda: point(p, 1))
+        point(p, 1)
+        factor_block(
+            [s_ref[m, p, p] for m in range(2)], u_ref, w_ref, r_ref,
+            lambda: point(p, 2), lambda: point(p, 3),
+        )
         for m in range(2):
             d_ref[m, p] = w_ref[m]
             s_ref[m, p, p] = u_ref[m]
-        point(p, 2)
+        cols = pl.ds(pl.multiple_of(p * T, T), T)
+
+        def left(i, c):
+            before = pl.ds(pl.multiple_of(i * T, T), T)
+            for m in range(2):
+                term = dot(bond_ref[m, :, before], s_ref[m, i, p], ((1,), (0,)))
+                bond_ref[m, :, cols] = bond_ref[m, :, cols] - term
+            return c
+
+        lax.fori_loop(0, p, left, 0)
+        for m in range(2):
+            value = dot(bond_ref[m, :, cols], d_ref[m, p], ((1,), (1,)))
+            bond_ref[m, :, cols] = value
+            iso_ref[m, :, cols] = value * root_ref[m, :1, :]
         return carry
 
     lax.fori_loop(0, NB, block, 0)
@@ -503,14 +524,6 @@
             for q in range(NZ):
                 trace = trace + jnp.where(lane16 == row16 + 16 * q, gfull[q, m, p * (p + 3) // 2], 0.0)
         scale = lax.rsqrt(jnp.full((1, T), jnp.sum(trace) / (NB * T) + 1e-6, jnp.float32))
-        solved = []
-        for j in range(NB):
-            value = bond_ref[m, :, T * j : T * j + T]
-            for i in range(j):
-                value = value - dot(solved[i], s_ref[m, i, j], ((1,), (0,)))
-            value = dot(value, d_ref[m, j], ((1,), (1,)))
-            solved.append(value)
-            iso_ref[m, :, T * j : T * j + T] = value * root_ref[m, :1, :]
         for p in range(NB):
             total = None
             for i in range(p, NB):

time: 153 us -> 151 us (0.987)
  Pallas kernels: 146 us -> 143 us
    pallas_call x1, Pallas kernels: 146 us -> 143 us  [site_step(): pl.pallas_call(bond_kernel, out_shape=(jax.ShapeDtypeStruct(site_block.sh...]
where the time goes in v6:
time: 151 us
  Pallas kernels  143 us (95%)
  local copies, waits for them, and re-layouts  6.71 us (4%)
    pallas_call x1, Pallas kernels, site_step(): pl.pallas_call(bond_kernel, out_shape=(jax.ShapeDtypeStruct(site_block.sh...  143 us
    unnamed x3, local copies, waits for them, and re-layouts  6.04 us

profile of v6, /device:TPU:2, one launch (start us, length us, event | category | flops | bytes accessed | tf_op | source)
XLA Modules:
  0.0 150.6 jit_solution(4621658995887689116)
XLA Ops:
  0.6 0.8 copy.10
  1.4 0.7 reshape.7.pairs_ref
  2.1 143.3 %bond.1 = (f32[2,256,512]{2,1,0:T(8,128)}, bf16[2,512,512]{2,1,0:T(8,128)(2,1)}) custom-call(s32[64]{0:T(128)} %owner_ref.1, s32[256]{0:T(256)} %reshape.7.pairs_ref, s32[64]{0:T(128)} %sizes_ref.1, s32[64]{0:T(128)} %charges_ref.1, bf16[2,4,2048,256]{3,2,1,0:T(8,128)(2,1)} %env_ref.1, bf16[2,256,512]{2,1,0:T(8,128)(2,1)} %block_ref.1, ...), custom_call_target="tpu_custom_call" | custom-call | tf_op jit(solution)/shard_map/bond/pallas_call | solution.py:543
  145.4 3.0 %copy.11 = f32[256,2,512]{2,1,0:T(2,128)} copy(f32[256,2,512]{2,0,1:T(8,128)} %bitcast.1) | data formatting | bytes 2097152
  148.4 2.3 %copy.13 = bf16[2,512,512]{2,1,0:T(8,128)(2,1)} copy(bf16[2,512,512]{2,1,0:T(8,128)(2,1)} %get-tuple-element.13) | data formatting | bytes 2097152

commit v7 on v6

--- a/solution.py
+++ b/solution.py
@@ -182,7 +182,7 @@
         fields.append(charges_ref[sectors[t]].astype(jnp.float32) * (2.0 / 64))
         root_ref[t] = jnp.sqrt(jnp.full((8, T), sizes_ref[sectors[t]], jnp.int32).astype(jnp.float32))
         for n in range(4):
-            place = owner_ref[pairs_ref[4 * sectors[t] + n]]
+            place = owner_ref[pairs_ref[sectors[t], n]]
             px, py, pc = (place // 4) % SIDE, place // (4 * SIDE), (place // 2) % 2
             even = (py * 2 + pc) * SIDE + px
             odd = 32 + (px * 2 + pc) * SIDE + py
@@ -588,7 +588,7 @@
 
 def local(environment, site_block, next_site, charges, sizes, pairs, owner):
     iso, advanced = site_step(
-        owner, pairs.reshape(-1), sizes, charges, environment, site_block, next_site
+        owner, pairs, sizes, charges, environment, site_block, next_site
     )
     return (jnp.swapaxes(iso, 0, 1), advanced)
 

time: 151 us -> 151 us (level)
  no operation moved by 1% of the time
where the time goes in v7:
time: 151 us
  Pallas kernels  143 us (95%)
  local copies, waits for them, and re-layouts  6.65 us (4%)
    pallas_call x1, Pallas kernels, site_step(): pl.pallas_call(bond_kernel, out_shape=(jax.ShapeDtypeStruct(site_block.sh...  143 us
    unnamed x3, local copies, waits for them, and re-layouts  6.65 us

profile of v7, /device:TPU:2, one launch (start us, length us, event | category | flops | bytes accessed | tf_op | source)
XLA Modules:
  0.0 150.7 jit_solution(16962861147480339404)
XLA Ops:
  0.6 1.4 copy.9.pairs_ref
  2.0 143.4 %bond.1 = (f32[2,256,512]{2,1,0:T(8,128)}, bf16[2,512,512]{2,1,0:T(8,128)(2,1)}) custom-call(s32[64]{0:T(128)} %owner_ref.1, s32[64,4]{1,0:T(8,128)} %copy.9.pairs_ref, s32[64]{0:T(128)} %sizes_ref.1, s32[64]{0:T(128)} %charges_ref.1, bf16[2,4,2048,256]{3,2,1,0:T(8,128)(2,1)} %env_ref.1, bf16[2,256,512]{2,1,0:T(8,128)(2,1)} %block_ref.1, ...), custom_call_target="tpu_custom_call" | custom-call | tf_op jit(solution)/shard_map/bond/pallas_call | solution.py:543
  145.5 3.0 %copy.10 = f32[256,2,512]{2,1,0:T(2,128)} copy(f32[256,2,512]{2,0,1:T(8,128)} %bitcast.1) | data formatting | bytes 2097152
  148.5 2.3 %copy.12 = bf16[2,512,512]{2,1,0:T(8,128)(2,1)} copy(bf16[2,512,512]{2,1,0:T(8,128)(2,1)} %get-tuple-element.11) | data formatting | bytes 2097152
